TPU v7x, 1024 devices: a whole 8x8x8 slice. The times are simulated.
1024 devices in a mesh: sec: 2 (over core), tile: 512 (over x, z, y).
Axes of the slice: x: 8, y: 8, z: 8, core: 2. Of those that a mesh axis runs over, the one named last changes fastest.
Arguments:
- velocity: float32 [3, 2048, 128, 128], P(None, 'tile', 'sec'), may hold values from -6 to 6
- stresses: float32 [6, 2048, 128, 128], P(None, 'tile', 'sec'), may hold values from -6 to 6
- buoyancy: float32 [2048, 128, 128], P('tile', 'sec'), may hold values from 0.5 to 1.5
- lame_first: float32 [2048, 128, 128], P('tile', 'sec'), may hold values from 0.5 to 1.5
- shear_mod: float32 [2048, 128, 128], P('tile', 'sec'), may hold values from 0.3 to 1
- ocean_state: float32 [3, 32768, 512], P(None, 'tile', 'sec'), may hold values from -6 to 6
- depth_map: float32 [32768, 512], P('tile', 'sec'), may hold values from 0.5 to 2
- wet_mask: int32 [32768, 512], P('tile', 'sec'), may hold values 0 or 1
- intersection_src: int32 [32768], P('tile'), may hold values from 0 to 511, as said below
- intersection_share: float32 [32768], P('tile'), may hold values from 0.3 to 1
Outputs:
- velocity_out: float32 [3, 2048, 128, 128], P(None, 'tile', 'sec')
- stress_out: float32 [6, 2048, 128, 128], P(None, 'tile', 'sec')
- ocean_out: float32 [3, 32768, 512], P(None, 'tile', 'sec')
Inputs may be any that keep to these rules, and one draw needn't show every extreme that they name: intersection_src[r] differs from r // 64 by at most 2.
All inputs are finite; a program needn't handle non-finite values. No bound on the sum of `wet_mask` on one device may be relied on, other than what follows from the above.
Results may differ from a plain program's by a relative error of at most 0.000096.
Values sent between devices are 32-bit elements; how exact they have to be, the bound alone decides.
A program may use at most 32 MiB of HBM per device.

v0:
```python
import jax
import jax.numpy as jnp
from jax import lax
from jax.sharding import PartitionSpec as P

STEPS = 2
OSTEPS = 2
REACH = 2


NEAR_COEF = 9.0 / 8.0
FAR_COEF = -1.0 / 24.0
TIME_STEP = 0.15
OCEAN_STEP = 0.3


def extended(cells, sides, width):
    for axis, dim in sides:
        count = lax.axis_size(axis)
        ends = count - 1
        head = lax.slice_in_dim(cells, 0, width, axis=dim)
        tail = lax.slice_in_dim(cells, cells.shape[dim] - width, cells.shape[dim], axis=dim)
        cells = jnp.concatenate(
            [
                lax.ppermute(tail, axis, [(i, (i + 1) % count) for i in range(ends)]),
                cells,
                lax.ppermute(head, axis, [((i + 1) % count, i) for i in range(ends)]),
            ],
            axis=dim,
        )
    return cells


def from_behind(value, axis, steps):
    count = lax.axis_size(axis)
    leading, last = (max(0, -steps), min(count, count - steps))
    return lax.ppermute(value, axis, [(source, source + steps) for source in range(leading, last)])


def offset_slice(field, shift, dimension):
    window = []
    for current in range(3):
        displaced = shift if current == dimension else 0
        window.append(slice(2 + displaced, field.shape[current] - 2 + displaced))
    return field[tuple(window)]


def forward_diff(field, dimension):
    return NEAR_COEF * (
        offset_slice(field, 1, dimension) - offset_slice(field, 0, dimension)
    ) + FAR_COEF * (offset_slice(field, 2, dimension) - offset_slice(field, -1, dimension))


def backward_diff(field, dimension):
    return NEAR_COEF * (
        offset_slice(field, 0, dimension) - offset_slice(field, -1, dimension)
    ) + FAR_COEF * (offset_slice(field, 1, dimension) - offset_slice(field, -2, dimension))


def update_velocity(velocity, stress_pad, buoyancy):
    accel_x = (
        forward_diff(stress_pad[0], 0)
        + backward_diff(stress_pad[3], 1)
        + backward_diff(stress_pad[4], 2)
    )
    accel_y = (
        backward_diff(stress_pad[3], 0)
        + forward_diff(stress_pad[1], 1)
        + backward_diff(stress_pad[5], 2)
    )
    accel_z = (
        backward_diff(stress_pad[4], 0)
        + backward_diff(stress_pad[5], 1)
        + forward_diff(stress_pad[2], 2)
    )
    return velocity + TIME_STEP * buoyancy * jnp.stack([accel_x, accel_y, accel_z])


def update_stress(stresses, velocity_pad, lame_first, shear_mod):
    strain_x = backward_diff(velocity_pad[0], 0)
    strain_y = backward_diff(velocity_pad[1], 1)
    strain_z = backward_diff(velocity_pad[2], 2)
    volume = strain_x + strain_y + strain_z
    normal_x = stresses[0] + TIME_STEP * (lame_first * volume + 2.0 * shear_mod * strain_x)
    normal_y = stresses[1] + TIME_STEP * (lame_first * volume + 2.0 * shear_mod * strain_y)
    normal_z = stresses[2] + TIME_STEP * (lame_first * volume + 2.0 * shear_mod * strain_z)
    shear_xy = stresses[3] + TIME_STEP * shear_mod * (
        forward_diff(velocity_pad[0], 1) + forward_diff(velocity_pad[1], 0)
    )
    shear_xz = stresses[4] + TIME_STEP * shear_mod * (
        forward_diff(velocity_pad[0], 2) + forward_diff(velocity_pad[2], 0)
    )
    shear_yz = stresses[5] + TIME_STEP * shear_mod * (
        forward_diff(velocity_pad[1], 2) + forward_diff(velocity_pad[2], 1)
    )
    return jnp.stack([normal_x, normal_y, normal_z, shear_xy, shear_xz, shear_yz])


def depth_pad(stacked):
    return jnp.pad(stacked, ((0, 0), (0, 0), (0, 0), (2, 2)))


def shards(
    velocity,
    stresses,
    buoyancy,
    lame_first,
    shear_mod,
    ocean_state,
    depth_map,
    wet_mask,
    intersection_src,
    intersection_share,
):
    for step_index in range(STEPS):
        stress_pad = depth_pad(extended(stresses, (("tile", 1), ("sec", 2)), 2))
        velocity = update_velocity(velocity, stress_pad, buoyancy)
        velocity_pad = depth_pad(extended(velocity, (("tile", 1), ("sec", 2)), 2))
        stresses = update_stress(stresses, velocity_pad, lame_first, shear_mod)
    patch = velocity[2, :, :, 0].reshape(-1)
    candidates = []
    for offset in range(-REACH, REACH + 1):
        if offset == 0:
            candidates.append(patch)
        else:
            candidates.append(from_behind(patch, "tile", -offset))
    candidates = jnp.stack(candidates)
    relative = intersection_src - lax.axis_index("tile") + REACH
    selector = (relative[:, None] == jnp.arange(2 * REACH + 1, dtype=jnp.int32)[None, :]).astype(
        jnp.float32
    )
    uplift = jnp.dot(
        selector, candidates, precision=lax.Precision.HIGHEST, preferred_element_type=jnp.float32
    )
    wet_float = wet_mask.astype(jnp.float32)
    source = intersection_share[:, None] * wet_float * uplift
    for step_index in range(OSTEPS):
        surface = ocean_state[0]
        padded = extended(surface, (("tile", 0), ("sec", 1)), 1)
        grad_x = (padded[2:, 1:-1] - padded[:-2, 1:-1]) * 0.5
        grad_y = (padded[1:-1, 2:] - padded[1:-1, :-2]) * 0.5
        flow_x = wet_float * (ocean_state[1] - OCEAN_STEP * grad_x)
        flow_y = wet_float * (ocean_state[2] - OCEAN_STEP * grad_y)
        flux_pad = extended(
            jnp.stack([depth_map * flow_x, depth_map * flow_y]), (("tile", 1), ("sec", 2)), 1
        )
        spread = (flux_pad[0, 2:, 1:-1] - flux_pad[0, :-2, 1:-1]) * 0.5 + (
            flux_pad[1, 1:-1, 2:] - flux_pad[1, 1:-1, :-2]
        ) * 0.5
        surface = surface - OCEAN_STEP * spread + OCEAN_STEP * source
        ocean_state = jnp.stack([surface, flow_x, flow_y])
    return (velocity, stresses, ocean_state)


def solution(mesh):
    return jax.shard_map(
        shards,
        mesh=mesh,
        in_specs=(
            P(None, "tile", "sec", None),
            P(None, "tile", "sec", None),
            P("tile", "sec", None),
            P("tile", "sec", None),
            P("tile", "sec", None),
            P(None, "tile", "sec"),
            P("tile", "sec"),
            P("tile", "sec"),
            P("tile"),
            P("tile"),
        ),
        out_specs=(
            P(None, "tile", "sec", None),
            P(None, "tile", "sec", None),
            P(None, "tile", "sec"),
        ),
        check_vma=False,
    )
```

profile of v0, /device:TPU:9, one launch (start us, length us, event | category | flops | bytes accessed | tf_op | source)
XLA Modules:
  0.0 187.7 jit_solution(10758809271428613401)
XLA Ops:
  0.6 1.2 fusion.200
  1.9 3.5 %collective-permute-start = (f32[6,2,64,128]{3,2,1,0:T(8,128)S(1)}, f32[6,2,64,128]{3,2,1,0:T(8,128)S(1)}, u32[]{:S(2)}, u32[]{:S(2)}) collective-permute-start(f32[6,2,64,128]{3,2,1,0:T(8,128)S(1)} %get-tuple-element.53), channel_id=1, source_target_pairs={{0,1},{1,2},{2,3},{3,4},{4,5},{5,6},{6,7},{7,8},{8,9},{9,10},{10,1... | collective-permute-start | bytes 1179656 | tf_op jit(solution)/shard_map/ppermute | solution.py:25
  5.4 19.3 %collective-permute-start.1 = (f32[6,2,64,128]{3,2,1,0:T(8,128)S(1)}, f32[6,2,64,128]{3,2,1,0:T(8,128)S(1)}, u32[]{:S(2)}, u32[]{:S(2)}) collective-permute-start(f32[6,2,64,128]{3,2,1,0:T(8,128)S(1)} %get-tuple-element.52), channel_id=1, source_target_pairs={{1,0},{2,1},{3,2},{4,3},{5,4},{6,5},{7,6},{8,7},{9,8},{10,9},{11,1... | collective-permute-start | bytes 1179656 | tf_op jit(solution)/shard_map/ppermute | solution.py:27
  24.7 0.7 slice_bitcast_fusion.19
  25.4 3.4 %collective-permute-start.16 = (f32[1,256]{1,0:T(1,128)S(1)}, f32[1,256]{1,0:T(1,128)S(1)}, u32[]{:S(2)}, u32[]{:S(2)}) collective-permute-start(f32[1,256]{1,0:T(1,128)S(1)} %get-tuple-element.60), channel_id=1, source_target_pairs={{1,0},{2,1},{3,2},{4,3},{5,4},{6,5},{7,6},{8,7},{9,8},{10,9},{11,1... | collective-permute-start | bytes 3080 | tf_op jit(solution)/shard_map/ppermute | solution.py:27
  28.8 1.9 %collective-permute-start.17 = (f32[1,256]{1,0:T(1,128)S(1)}, f32[1,256]{1,0:T(1,128)S(1)}, u32[]{:S(2)}, u32[]{:S(2)}) collective-permute-start(f32[1,256]{1,0:T(1,128)S(1)} %get-tuple-element.59), channel_id=1, source_target_pairs={{0,1},{1,2},{2,3},{3,4},{4,5},{5,6},{6,7},{7,8},{8,9},{9,10},{10,1... | collective-permute-start | bytes 3080 | tf_op jit(solution)/shard_map/ppermute | solution.py:25
  30.7 0.9 collective-permute-done
  31.7 0.8 collective-permute-done.1
  32.5 1.3 collective-permute-start.2
  33.8 3.5 %collective-permute-start.3 = (f32[6,8,2,128]{3,2,1,0:T(2,128)S(1)}, f32[6,8,2,128]{3,2,1,0:T(2,128)S(1)}, u32[]{:S(2)}, u32[]{:S(2)}) collective-permute-start(f32[6,8,2,128]{3,2,1,0:T(2,128)S(1)} %get-tuple-element.45), channel_id=1, source_target_pairs={{512,0},{513,1},{514,2},{515,3},{516,4},{517,5},{518,6},{519,7},{5... | collective-permute-start | bytes 147464 | tf_op jit(solution)/shard_map/ppermute | solution.py:27
  37.3 0.8 collective-permute-done.3
  38.2 1.3 select_maximum_fusion.4
  41.3 1.9 %collective-permute-start.4 = (f32[3,2,64,128]{3,2,1,0:T(8,128)S(1)}, f32[3,2,64,128]{3,2,1,0:T(8,128)S(1)}, u32[]{:S(2)}, u32[]{:S(2)}) collective-permute-start(f32[3,2,64,128]{3,2,1,0:T(8,128)S(1)} %get-tuple-element.57), channel_id=1, source_target_pairs={{0,1},{1,2},{2,3},{3,4},{4,5},{5,6},{6,7},{7,8},{8,9},{9,10},{10,1... | collective-permute-start | bytes 589832 | tf_op jit(solution)/shard_map/ppermute | solution.py:25
  43.2 9.5 %collective-permute-start.5 = (f32[3,2,64,128]{3,2,1,0:T(8,128)S(1)}, f32[3,2,64,128]{3,2,1,0:T(8,128)S(1)}, u32[]{:S(2)}, u32[]{:S(2)}) collective-permute-start(f32[3,2,64,128]{3,2,1,0:T(8,128)S(1)} %get-tuple-element.58), channel_id=1, source_target_pairs={{1,0},{2,1},{3,2},{4,3},{5,4},{6,5},{7,6},{8,7},{9,8},{10,9},{11,1... | collective-permute-start | bytes 589832 | tf_op jit(solution)/shard_map/ppermute | solution.py:27
  52.8 3.0 %collective-permute-done.4 = f32[3,2,64,128]{3,2,1,0:T(8,128)S(1)} collective-permute-done((f32[3,2,64,128]{3,2,1,0:T(8,128)S(1)}, f32[3,2,64,128]{3,2,1,0:T(8,128)S(1)}, u32[]{:S(2)}, u32[]{:S(2)}) %collective-permute-start.4) | collective-permute-done | bytes 196640 | tf_op jit(solution)/shard_map/ppermute | solution.py:25
  55.8 0.9 collective-permute-done.5
  56.7 1.3 collective-permute-start.6
  58.0 3.1 %collective-permute-start.7 = (f32[3,8,2,128]{3,2,1,0:T(2,128)S(1)}, f32[3,8,2,128]{3,2,1,0:T(2,128)S(1)}, u32[]{:S(2)}, u32[]{:S(2)}) collective-permute-start(f32[3,8,2,128]{3,2,1,0:T(2,128)S(1)} %get-tuple-element.51), channel_id=1, source_target_pairs={{512,0},{513,1},{514,2},{515,3},{516,4},{517,5},{518,6},{519,7},{5... | collective-permute-start | bytes 73736 | tf_op jit(solution)/shard_map/ppermute | solution.py:27
  61.1 1.3 collective-permute-start.18
  62.4 1.3 collective-permute-start.19
  63.8 0.6 select_maximum_fusion.10
  64.5 0.8 copy-done
  65.4 1.1 bitcast_dynamic-update-slice_fusion.8
  67.7 1.9 %collective-permute-start.8 = (f32[6,2,64,128]{3,2,1,0:T(8,128)S(1)}, f32[6,2,64,128]{3,2,1,0:T(8,128)S(1)}, u32[]{:S(2)}, u32[]{:S(2)}) collective-permute-start(f32[6,2,64,128]{3,2,1,0:T(8,128)S(1)} %get-tuple-element.48), channel_id=1, source_target_pairs={{0,1},{1,2},{2,3},{3,4},{4,5},{5,6},{6,7},{7,8},{8,9},{9,10},{10,1... | collective-permute-start | bytes 1179656 | tf_op jit(solution)/shard_map/ppermute | solution.py:25
  69.6 9.5 %collective-permute-start.9 = (f32[6,2,64,128]{3,2,1,0:T(8,128)S(1)}, f32[6,2,64,128]{3,2,1,0:T(8,128)S(1)}, u32[]{:S(2)}, u32[]{:S(2)}) collective-permute-start(f32[6,2,64,128]{3,2,1,0:T(8,128)S(1)} %get-tuple-element.49), channel_id=1, source_target_pairs={{1,0},{2,1},{3,2},{4,3},{5,4},{6,5},{7,6},{8,7},{9,8},{10,9},{11,1... | collective-permute-start | bytes 1179656 | tf_op jit(solution)/shard_map/ppermute | solution.py:27
  79.2 0.6 subtract_add_fusion
  79.8 0.8 multiply_bitcast_fusion.2
  80.5 3.4 %collective-permute-start.20 = (f32[2,1,256]{2,1,0:T(1,128)S(1)}, f32[2,1,256]{2,1,0:T(1,128)S(1)}, u32[]{:S(2)}, u32[]{:S(2)}) collective-permute-start(f32[2,1,256]{2,1,0:T(1,128)S(1)} %get-tuple-element.68), channel_id=1, source_target_pairs={{1,0},{2,1},{3,2},{4,3},{5,4},{6,5},{7,6},{8,7},{9,8},{10,9},{11,1... | collective-permute-start | bytes 6152 | tf_op jit(solution)/shard_map/ppermute | solution.py:27
  83.9 1.9 %collective-permute-start.21 = (f32[2,1,256]{2,1,0:T(1,128)S(1)}, f32[2,1,256]{2,1,0:T(1,128)S(1)}, u32[]{:S(2)}, u32[]{:S(2)}) collective-permute-start(f32[2,1,256]{2,1,0:T(1,128)S(1)} %get-tuple-element.67), channel_id=1, source_target_pairs={{0,1},{1,2},{2,3},{3,4},{4,5},{5,6},{6,7},{7,8},{8,9},{9,10},{10,1... | collective-permute-start | bytes 6152 | tf_op jit(solution)/shard_map/ppermute | solution.py:25
  85.8 0.6 collective-permute-done.9
  86.4 1.3 collective-permute-start.10
  87.7 4.0 %collective-permute-start.11 = (f32[6,8,2,128]{3,2,1,0:T(2,128)S(1)}, f32[6,8,2,128]{3,2,1,0:T(2,128)S(1)}, u32[]{:S(2)}, u32[]{:S(2)}) collective-permute-start(f32[6,8,2,128]{3,2,1,0:T(2,128)S(1)} %get-tuple-element.43), channel_id=1, source_target_pairs={{512,0},{513,1},{514,2},{515,3},{516,4},{517,5},{518,6},{519,7},{5... | collective-permute-start | bytes 147464 | tf_op jit(solution)/shard_map/ppermute | solution.py:27
  91.8 1.9 %collective-permute-done.21 = f32[2,1,256]{2,1,0:T(1,128)S(1)} collective-permute-done((f32[2,1,256]{2,1,0:T(1,128)S(1)}, f32[2,1,256]{2,1,0:T(1,128)S(1)}, u32[]{:S(2)}, u32[]{:S(2)}) %collective-permute-start.21) | collective-permute-done | bytes 2080 | tf_op jit(solution)/shard_map/ppermute | solution.py:25
  94.2 2.1 %select_maximum_fusion = f32[6,8,68,132]{3,2,1,0:T(8,128)S(1)} fusion(f32[6,8,2,128]{3,2,1,0:T(2,128)S(1)} %collective-permute-done.11, f32[6,8,2,128]{3,2,1,0:T(2,128)S(1)} %collective-permute-done.10, f32[6,2,64,128]{3,2,1,0:T(8,128)S(1)} %collective-permute-done.9, f32[6,4,64,128]{3,2,1,0:T(8,128)S(1)} %get-tuple-element.13, ...), kind=kLoop, calls=%fused_computation.2 | loop fusion | flops 5170176 | bytes 3394560 | tf_op jit(solution)/shard_map/concatenate | solution.py:23
  98.5 1.9 %collective-permute-start.24 = (f32[256]{0:T(256)S(1)}, f32[256]{0:T(256)S(1)}, u32[]{:S(2)}, u32[]{:S(2)}) collective-permute-start(f32[256]{0:T(256)S(1)} %reshape_squeeze.3), channel_id=1, source_target_pairs={{0,2},{1,3},{2,4},{3,5},{4,6},{5,7},{6,8},{7,9},{8,10},{9,11},{10,... | collective-permute-start | bytes 3080 | tf_op jit(solution)/shard_map/ppermute | solution.py:37
  100.4 1.9 %collective-permute-start.25 = (f32[256]{0:T(256)S(1)}, f32[256]{0:T(256)S(1)}, u32[]{:S(2)}, u32[]{:S(2)}) collective-permute-start(f32[256]{0:T(256)S(1)} %reshape_squeeze.3), channel_id=1, source_target_pairs={{0,1},{1,2},{2,3},{3,4},{4,5},{5,6},{6,7},{7,8},{8,9},{9,10},{10,1... | collective-permute-start | bytes 3080 | tf_op jit(solution)/shard_map/ppermute | solution.py:37
  102.3 8.8 %collective-permute-start.26 = (f32[256]{0:T(256)S(1)}, f32[256]{0:T(256)S(1)}, u32[]{:S(2)}, u32[]{:S(2)}) collective-permute-start(f32[256]{0:T(256)S(1)} %reshape_squeeze.3), channel_id=1, source_target_pairs={{1,0},{2,1},{3,2},{4,3},{5,4},{6,5},{7,6},{8,7},{9,8},{10,9},{11,1... | collective-permute-start | bytes 3080 | tf_op jit(solution)/shard_map/ppermute | solution.py:37
  111.1 4.3 %collective-permute-start.27 = (f32[256]{0:T(256)S(1)}, f32[256]{0:T(256)S(1)}, u32[]{:S(2)}, u32[]{:S(2)}) collective-permute-start(f32[256]{0:T(256)S(1)} %reshape_squeeze.3), channel_id=1, source_target_pairs={{2,0},{3,1},{4,2},{5,3},{6,4},{7,5},{8,6},{9,7},{10,8},{11,9},{12,... | collective-permute-start | bytes 3080 | tf_op jit(solution)/shard_map/ppermute | solution.py:37
  115.5 6.1 %collective-permute-start.22 = (f32[2,66,1]{2,1,0:T(8,128)S(1)}, f32[2,66,1]{2,1,0:T(8,128)S(1)}, u32[]{:S(2)}, u32[]{:S(2)}) collective-permute-start(f32[2,66,1]{2,1,0:T(8,128)S(1)} %get-tuple-element.63), channel_id=1, source_target_pairs={{512,0},{513,1},{514,2},{515,3},{516,4},{517,5},{518,6},{519,7},{5... | collective-permute-start | bytes 1592 | tf_op jit(solution)/shard_map/ppermute | solution.py:27
  121.6 1.3 collective-permute-start.23
  123.1 1.7 collective-permute-done.23
  124.8 1.1 fusion.176
  125.9 1.9 %collective-permute-start.28 = (f32[1,256]{1,0:T(1,128)S(1)}, f32[1,256]{1,0:T(1,128)S(1)}, u32[]{:S(2)}, u32[]{:S(2)}) collective-permute-start(f32[1,256]{1,0:T(1,128)S(1)} %get-tuple-element.74), channel_id=1, source_target_pairs={{1,0},{2,1},{3,2},{4,3},{5,4},{6,5},{7,6},{8,7},{9,8},{10,9},{11,1... | collective-permute-start | bytes 3080 | tf_op jit(solution)/shard_map/ppermute | solution.py:27
  127.8 3.4 %collective-permute-start.29 = (f32[1,256]{1,0:T(1,128)S(1)}, f32[1,256]{1,0:T(1,128)S(1)}, u32[]{:S(2)}, u32[]{:S(2)}) collective-permute-start(f32[1,256]{1,0:T(1,128)S(1)} %get-tuple-element.73), channel_id=1, source_target_pairs={{0,1},{1,2},{2,3},{3,4},{4,5},{5,6},{6,7},{7,8},{8,9},{9,10},{10,1... | collective-permute-start | bytes 3080 | tf_op jit(solution)/shard_map/ppermute | solution.py:25
  131.2 6.4 %collective-permute-done.29 = f32[1,256]{1,0:T(1,128)S(1)} collective-permute-done((f32[1,256]{1,0:T(1,128)S(1)}, f32[1,256]{1,0:T(1,128)S(1)}, u32[]{:S(2)}, u32[]{:S(2)}) %collective-permute-start.29) | collective-permute-done | bytes 1056 | tf_op jit(solution)/shard_map/ppermute | solution.py:25
  137.7 6.3 %collective-permute-start.30 = (f32[66,1]{1,0:T(8,128)S(1)}, f32[66,1]{1,0:T(8,128)S(1)}, u32[]{:S(2)}, u32[]{:S(2)}) collective-permute-start(f32[66,1]{1,0:T(8,128)S(1)} %get-tuple-element.69), channel_id=1, source_target_pairs={{512,0},{513,1},{514,2},{515,3},{516,4},{517,5},{518,6},{519,7},{5... | collective-permute-start | bytes 800 | tf_op jit(solution)/shard_map/ppermute | solution.py:27
  144.0 1.3 collective-permute-start.31
  145.3 0.9 multiply_bitcast_fusion.1
  146.2 0.9 collective-permute-done.31
  147.3 1.9 %collective-permute-start.32 = (f32[2,1,256]{2,1,0:T(1,128)S(1)}, f32[2,1,256]{2,1,0:T(1,128)S(1)}, u32[]{:S(2)}, u32[]{:S(2)}) collective-permute-start(f32[2,1,256]{2,1,0:T(1,128)S(1)} %get-tuple-element.66), channel_id=1, source_target_pairs={{1,0},{2,1},{3,2},{4,3},{5,4},{6,5},{7,6},{8,7},{9,8},{10,9},{11,1... | collective-permute-start | bytes 6152 | tf_op jit(solution)/shard_map/ppermute | solution.py:27
  149.2 3.4 %collective-permute-start.33 = (f32[2,1,256]{2,1,0:T(1,128)S(1)}, f32[2,1,256]{2,1,0:T(1,128)S(1)}, u32[]{:S(2)}, u32[]{:S(2)}) collective-permute-start(f32[2,1,256]{2,1,0:T(1,128)S(1)} %get-tuple-element.65), channel_id=1, source_target_pairs={{0,1},{1,2},{2,3},{3,4},{4,5},{5,6},{6,7},{7,8},{8,9},{9,10},{10,1... | collective-permute-start | bytes 6152 | tf_op jit(solution)/shard_map/ppermute | solution.py:25
  152.6 6.4 %collective-permute-done.33 = f32[2,1,256]{2,1,0:T(1,128)S(1)} collective-permute-done((f32[2,1,256]{2,1,0:T(1,128)S(1)}, f32[2,1,256]{2,1,0:T(1,128)S(1)}, u32[]{:S(2)}, u32[]{:S(2)}) %collective-permute-start.33) | collective-permute-done | bytes 2080 | tf_op jit(solution)/shard_map/ppermute | solution.py:25
  159.0 3.3 %collective-permute-start.34 = (f32[2,66,1]{2,1,0:T(8,128)S(1)}, f32[2,66,1]{2,1,0:T(8,128)S(1)}, u32[]{:S(2)}, u32[]{:S(2)}) collective-permute-start(f32[2,66,1]{2,1,0:T(8,128)S(1)} %get-tuple-element.61), channel_id=1, source_target_pairs={{512,0},{513,1},{514,2},{515,3},{516,4},{517,5},{518,6},{519,7},{5... | collective-permute-start | bytes 1592 | tf_op jit(solution)/shard_map/ppermute | solution.py:27
  162.4 1.3 collective-permute-start.35
  163.7 1.9 %collective-permute-start.12 = (f32[3,2,64,128]{3,2,1,0:T(8,128)S(1)}, f32[3,2,64,128]{3,2,1,0:T(8,128)S(1)}, u32[]{:S(2)}, u32[]{:S(2)}) collective-permute-start(f32[3,2,64,128]{3,2,1,0:T(8,128)S(1)} %get-tuple-element.55), channel_id=1, source_target_pairs={{0,1},{1,2},{2,3},{3,4},{4,5},{5,6},{6,7},{7,8},{8,9},{9,10},{10,1... | collective-permute-start | bytes 589832 | tf_op jit(solution)/shard_map/ppermute | solution.py:25
  165.6 9.0 %collective-permute-start.13 = (f32[3,2,64,128]{3,2,1,0:T(8,128)S(1)}, f32[3,2,64,128]{3,2,1,0:T(8,128)S(1)}, u32[]{:S(2)}, u32[]{:S(2)}) collective-permute-start(f32[3,2,64,128]{3,2,1,0:T(8,128)S(1)} %get-tuple-element.56), channel_id=1, source_target_pairs={{1,0},{2,1},{3,2},{4,3},{5,4},{6,5},{7,6},{8,7},{9,8},{10,9},{11,1... | collective-permute-start | bytes 589832 | tf_op jit(solution)/shard_map/ppermute | solution.py:27
  174.8 1.5 collective-permute-done.12
  176.3 0.7 collective-permute-done.13
  177.0 1.3 collective-permute-start.14
  178.3 4.4 %collective-permute-start.15 = (f32[3,8,2,128]{3,2,1,0:T(2,128)S(1)}, f32[3,8,2,128]{3,2,1,0:T(2,128)S(1)}, u32[]{:S(2)}, u32[]{:S(2)}) collective-permute-start(f32[3,8,2,128]{3,2,1,0:T(2,128)S(1)} %get-tuple-element.47), channel_id=1, source_target_pairs={{512,0},{513,1},{514,2},{515,3},{516,4},{517,5},{518,6},{519,7},{5... | collective-permute-start | bytes 73736 | tf_op jit(solution)/shard_map/ppermute | solution.py:27
  182.8 0.7 pad_maximum_fusion
  183.6 0.6 select_maximum_fusion.6
  184.4 0.7 copy-done.7
  186.8 0.9 copy-done.12
  (108 shorter events, 8.7 us)
Async XLA Ops:
  0.6 31.0 %copy-start.1 = (f32[6,4,64,128]{3,2,1,0:T(8,128)S(1)}, f32[6,4,64,128]{3,2,1,0:T(8,128)}, u32[]{:S(2)}) copy-start(f32[6,4,64,128]{3,2,1,0:T(8,128)} %param.11) | copy-start | bytes 2359300
  1.9 35.4 %copy-start.11 = (f32[4,64,128]{2,1,0:T(8,128)S(1)}, f32[4,64,128]{2,1,0:T(8,128)}, u32[]{:S(2)}) copy-start(f32[4,64,128]{2,1,0:T(8,128)} %param.12) | copy-start | bytes 393220
  1.9 29.7 %collective-permute-start = (f32[6,2,64,128]{3,2,1,0:T(8,128)S(1)}, f32[6,2,64,128]{3,2,1,0:T(8,128)S(1)}, u32[]{:S(2)}, u32[]{:S(2)}) collective-permute-start(f32[6,2,64,128]{3,2,1,0:T(8,128)S(1)} %get-tuple-element.53), channel_id=1, source_target_pairs={{0,1},{1,2},{2,3},{3,4},{4,5},{5,6},{6,7},{7,8},{8,9},{9,10},{10,1... | collective-permute-start | bytes 1179656 | tf_op jit(solution)/shard_map/ppermute | solution.py:25
  5.4 27.1 %collective-permute-start.1 = (f32[6,2,64,128]{3,2,1,0:T(8,128)S(1)}, f32[6,2,64,128]{3,2,1,0:T(8,128)S(1)}, u32[]{:S(2)}, u32[]{:S(2)}) collective-permute-start(f32[6,2,64,128]{3,2,1,0:T(8,128)S(1)} %get-tuple-element.52), channel_id=1, source_target_pairs={{1,0},{2,1},{3,2},{4,3},{5,4},{6,5},{7,6},{8,7},{9,8},{10,9},{11,1... | collective-permute-start | bytes 1179656 | tf_op jit(solution)/shard_map/ppermute | solution.py:27
  25.4 27.4 %collective-permute-start.16 = (f32[1,256]{1,0:T(1,128)S(1)}, f32[1,256]{1,0:T(1,128)S(1)}, u32[]{:S(2)}, u32[]{:S(2)}) collective-permute-start(f32[1,256]{1,0:T(1,128)S(1)} %get-tuple-element.60), channel_id=1, source_target_pairs={{1,0},{2,1},{3,2},{4,3},{5,4},{6,5},{7,6},{8,7},{9,8},{10,9},{11,1... | collective-permute-start | bytes 3080 | tf_op jit(solution)/shard_map/ppermute | solution.py:27
  28.8 24.0 %collective-permute-start.17 = (f32[1,256]{1,0:T(1,128)S(1)}, f32[1,256]{1,0:T(1,128)S(1)}, u32[]{:S(2)}, u32[]{:S(2)}) collective-permute-start(f32[1,256]{1,0:T(1,128)S(1)} %get-tuple-element.59), channel_id=1, source_target_pairs={{0,1},{1,2},{2,3},{3,4},{4,5},{5,6},{6,7},{7,8},{8,9},{9,10},{10,1... | collective-permute-start | bytes 3080 | tf_op jit(solution)/shard_map/ppermute | solution.py:25
  32.5 4.8 %collective-permute-start.2 = (f32[6,8,2,128]{3,2,1,0:T(2,128)S(1)}, f32[6,8,2,128]{3,2,1,0:T(2,128)S(1)}, u32[]{:S(2)}, u32[]{:S(2)}) collective-permute-start(f32[6,8,2,128]{3,2,1,0:T(2,128)S(1)} %get-tuple-element.44), channel_id=1, source_target_pairs={{0,512},{1,513},{2,514},{3,515},{4,516},{5,517},{6,518},{7,519},{8... | collective-permute-start | bytes 147464 | tf_op jit(solution)/shard_map/ppermute | solution.py:25
  33.8 4.3 %collective-permute-start.3 = (f32[6,8,2,128]{3,2,1,0:T(2,128)S(1)}, f32[6,8,2,128]{3,2,1,0:T(2,128)S(1)}, u32[]{:S(2)}, u32[]{:S(2)}) collective-permute-start(f32[6,8,2,128]{3,2,1,0:T(2,128)S(1)} %get-tuple-element.45), channel_id=1, source_target_pairs={{512,0},{513,1},{514,2},{515,3},{516,4},{517,5},{518,6},{519,7},{5... | collective-permute-start | bytes 147464 | tf_op jit(solution)/shard_map/ppermute | solution.py:27
  40.2 1.0 copy-start.3
  40.6 12.1 %copy-start.9 = (f32[3,64,256]{2,1,0:T(8,128)S(1)}, f32[3,64,256]{2,1,0:T(8,128)}, u32[]{:S(2)}) copy-start(f32[3,64,256]{2,1,0:T(8,128)} %param.15) | copy-start | bytes 589828
  41.3 14.5 %collective-permute-start.4 = (f32[3,2,64,128]{3,2,1,0:T(8,128)S(1)}, f32[3,2,64,128]{3,2,1,0:T(8,128)S(1)}, u32[]{:S(2)}, u32[]{:S(2)}) collective-permute-start(f32[3,2,64,128]{3,2,1,0:T(8,128)S(1)} %get-tuple-element.57), channel_id=1, source_target_pairs={{0,1},{1,2},{2,3},{3,4},{4,5},{5,6},{6,7},{7,8},{8,9},{9,10},{10,1... | collective-permute-start | bytes 589832 | tf_op jit(solution)/shard_map/ppermute | solution.py:25
  43.2 13.5 %collective-permute-start.5 = (f32[3,2,64,128]{3,2,1,0:T(8,128)S(1)}, f32[3,2,64,128]{3,2,1,0:T(8,128)S(1)}, u32[]{:S(2)}, u32[]{:S(2)}) collective-permute-start(f32[3,2,64,128]{3,2,1,0:T(8,128)S(1)} %get-tuple-element.58), channel_id=1, source_target_pairs={{1,0},{2,1},{3,2},{4,3},{5,4},{6,5},{7,6},{8,7},{9,8},{10,9},{11,1... | collective-permute-start | bytes 589832 | tf_op jit(solution)/shard_map/ppermute | solution.py:27
  52.8 27.0 %copy-start.13 = (f32[1,256]{1,0:T(1,128)}, f32[1,256]{1,0:T(1,128)S(1)}, u32[]{:S(2)}) copy-start(f32[1,256]{1,0:T(1,128)S(1)} %collective-permute-done.16) | copy-start | bytes 3076
  52.8 27.0 %copy-start.14 = (f32[1,256]{1,0:T(1,128)}, f32[1,256]{1,0:T(1,128)S(1)}, u32[]{:S(2)}) copy-start(f32[1,256]{1,0:T(1,128)S(1)} %collective-permute-done.17) | copy-start | bytes 3076
  56.7 7.1 %collective-permute-start.6 = (f32[3,8,2,128]{3,2,1,0:T(2,128)S(1)}, f32[3,8,2,128]{3,2,1,0:T(2,128)S(1)}, u32[]{:S(2)}, u32[]{:S(2)}) collective-permute-start(f32[3,8,2,128]{3,2,1,0:T(2,128)S(1)} %get-tuple-element.50), channel_id=1, source_target_pairs={{0,512},{1,513},{2,514},{3,515},{4,516},{5,517},{6,518},{7,519},{8... | collective-permute-start | bytes 73736 | tf_op jit(solution)/shard_map/ppermute | solution.py:25
  58.0 5.8 %collective-permute-start.7 = (f32[3,8,2,128]{3,2,1,0:T(2,128)S(1)}, f32[3,8,2,128]{3,2,1,0:T(2,128)S(1)}, u32[]{:S(2)}, u32[]{:S(2)}) collective-permute-start(f32[3,8,2,128]{3,2,1,0:T(2,128)S(1)} %get-tuple-element.51), channel_id=1, source_target_pairs={{512,0},{513,1},{514,2},{515,3},{516,4},{517,5},{518,6},{519,7},{5... | collective-permute-start | bytes 73736 | tf_op jit(solution)/shard_map/ppermute | solution.py:27
  61.1 18.6 %collective-permute-start.18 = (f32[66,1]{1,0:T(8,128)S(1)}, f32[66,1]{1,0:T(8,128)S(1)}, u32[]{:S(2)}, u32[]{:S(2)}) collective-permute-start(f32[66,1]{1,0:T(8,128)S(1)} %get-tuple-element.71), channel_id=1, source_target_pairs={{512,0},{513,1},{514,2},{515,3},{516,4},{517,5},{518,6},{519,7},{5... | collective-permute-start | bytes 800 | tf_op jit(solution)/shard_map/ppermute | solution.py:27
  62.4 17.3 %collective-permute-start.19 = (f32[66,1]{1,0:T(8,128)S(1)}, f32[66,1]{1,0:T(8,128)S(1)}, u32[]{:S(2)}, u32[]{:S(2)}) collective-permute-start(f32[66,1]{1,0:T(8,128)S(1)} %get-tuple-element.72), channel_id=1, source_target_pairs={{0,512},{1,513},{2,514},{3,515},{4,516},{5,517},{6,518},{7,519},{8... | collective-permute-start | bytes 800 | tf_op jit(solution)/shard_map/ppermute | solution.py:25
  64.4 0.9 copy-start
  64.4 1.0 copy-start.6
  67.2 11.9 %copy-start.17 = (s32[64]{0:T(128)S(1)}, s32[64]{0:T(128)}, u32[]{:S(2)}) copy-start(s32[64]{0:T(128)} %param.18) | copy-start | bytes 772
  67.2 12.5 %copy-start.4 = (f32[64,256]{1,0:T(8,128)S(1)}, f32[64,256]{1,0:T(8,128)}, u32[]{:S(2)}) copy-start(f32[64,256]{1,0:T(8,128)} %param.16) | copy-start | bytes 196612
  67.3 12.5 %copy-start.5 = (s32[64,256]{1,0:T(8,128)S(1)}, s32[64,256]{1,0:T(8,128)}, u32[]{:S(2)}) copy-start(s32[64,256]{1,0:T(8,128)} %param.17) | copy-start | bytes 196612
  67.7 18.2 %collective-permute-start.8 = (f32[6,2,64,128]{3,2,1,0:T(8,128)S(1)}, f32[6,2,64,128]{3,2,1,0:T(8,128)S(1)}, u32[]{:S(2)}, u32[]{:S(2)}) collective-permute-start(f32[6,2,64,128]{3,2,1,0:T(8,128)S(1)} %get-tuple-element.48), channel_id=1, source_target_pairs={{0,1},{1,2},{2,3},{3,4},{4,5},{5,6},{6,7},{7,8},{8,9},{9,10},{10,1... | collective-permute-start | bytes 1179656 | tf_op jit(solution)/shard_map/ppermute | solution.py:25
  69.6 16.8 %collective-permute-start.9 = (f32[6,2,64,128]{3,2,1,0:T(8,128)S(1)}, f32[6,2,64,128]{3,2,1,0:T(8,128)S(1)}, u32[]{:S(2)}, u32[]{:S(2)}) collective-permute-start(f32[6,2,64,128]{3,2,1,0:T(8,128)S(1)} %get-tuple-element.49), channel_id=1, source_target_pairs={{1,0},{2,1},{3,2},{4,3},{5,4},{6,5},{7,6},{8,7},{9,8},{10,9},{11,1... | collective-permute-start | bytes 1179656 | tf_op jit(solution)/shard_map/ppermute | solution.py:27
  80.5 11.2 %collective-permute-start.20 = (f32[2,1,256]{2,1,0:T(1,128)S(1)}, f32[2,1,256]{2,1,0:T(1,128)S(1)}, u32[]{:S(2)}, u32[]{:S(2)}) collective-permute-start(f32[2,1,256]{2,1,0:T(1,128)S(1)} %get-tuple-element.68), channel_id=1, source_target_pairs={{1,0},{2,1},{3,2},{4,3},{5,4},{6,5},{7,6},{8,7},{9,8},{10,9},{11,1... | collective-permute-start | bytes 6152 | tf_op jit(solution)/shard_map/ppermute | solution.py:27
  83.9 9.8 %collective-permute-start.21 = (f32[2,1,256]{2,1,0:T(1,128)S(1)}, f32[2,1,256]{2,1,0:T(1,128)S(1)}, u32[]{:S(2)}, u32[]{:S(2)}) collective-permute-start(f32[2,1,256]{2,1,0:T(1,128)S(1)} %get-tuple-element.67), channel_id=1, source_target_pairs={{0,1},{1,2},{2,3},{3,4},{4,5},{5,6},{6,7},{7,8},{8,9},{9,10},{10,1... | collective-permute-start | bytes 6152 | tf_op jit(solution)/shard_map/ppermute | solution.py:25
  86.4 7.2 %collective-permute-start.10 = (f32[6,8,2,128]{3,2,1,0:T(2,128)S(1)}, f32[6,8,2,128]{3,2,1,0:T(2,128)S(1)}, u32[]{:S(2)}, u32[]{:S(2)}) collective-permute-start(f32[6,8,2,128]{3,2,1,0:T(2,128)S(1)} %get-tuple-element.42), channel_id=1, source_target_pairs={{0,512},{1,513},{2,514},{3,515},{4,516},{5,517},{6,518},{7,519},{8... | collective-permute-start | bytes 147464 | tf_op jit(solution)/shard_map/ppermute | solution.py:25
  87.7 6.0 %collective-permute-start.11 = (f32[6,8,2,128]{3,2,1,0:T(2,128)S(1)}, f32[6,8,2,128]{3,2,1,0:T(2,128)S(1)}, u32[]{:S(2)}, u32[]{:S(2)}) collective-permute-start(f32[6,8,2,128]{3,2,1,0:T(2,128)S(1)} %get-tuple-element.43), channel_id=1, source_target_pairs={{512,0},{513,1},{514,2},{515,3},{516,4},{517,5},{518,6},{519,7},{5... | collective-permute-start | bytes 147464 | tf_op jit(solution)/shard_map/ppermute | solution.py:27
  91.7 2.0 %copy-start.15 = (f32[2,1,256]{2,1,0:T(1,128)}, f32[2,1,256]{2,1,0:T(1,128)S(1)}, u32[]{:S(2)}) copy-start(f32[2,1,256]{2,1,0:T(1,128)S(1)} %collective-permute-done.20) | copy-start | bytes 6148
  93.7 0.6 copy-start.16
  98.1 49.0 %copy-start.10 = (f32[64,256]{1,0:T(8,128)S(1)}, f32[64,256]{1,0:T(8,128)}, u32[]{:S(2)}) copy-start(f32[64,256]{1,0:T(8,128)} %get-tuple-element.8) | copy-start | bytes 196612
  98.3 85.3 %copy-start.2 = (f32[3,4,64,128]{3,2,1,0:T(8,128)}, f32[3,4,64,128]{3,2,1,0:T(8,128)S(1)}, u32[]{:S(2)}) copy-start(f32[3,4,64,128]{3,2,1,0:T(8,128)S(1)} %fusion.4) | copy-start | bytes 1179652
  98.5 23.2 %collective-permute-start.24 = (f32[256]{0:T(256)S(1)}, f32[256]{0:T(256)S(1)}, u32[]{:S(2)}, u32[]{:S(2)}) collective-permute-start(f32[256]{0:T(256)S(1)} %reshape_squeeze.3), channel_id=1, source_target_pairs={{0,2},{1,3},{2,4},{3,5},{4,6},{5,7},{6,8},{7,9},{8,10},{9,11},{10,... | collective-permute-start | bytes 3080 | tf_op jit(solution)/shard_map/ppermute | solution.py:37
  100.4 22.6 %collective-permute-start.25 = (f32[256]{0:T(256)S(1)}, f32[256]{0:T(256)S(1)}, u32[]{:S(2)}, u32[]{:S(2)}) collective-permute-start(f32[256]{0:T(256)S(1)} %reshape_squeeze.3), channel_id=1, source_target_pairs={{0,1},{1,2},{2,3},{3,4},{4,5},{5,6},{6,7},{7,8},{8,9},{9,10},{10,1... | collective-permute-start | bytes 3080 | tf_op jit(solution)/shard_map/ppermute | solution.py:37
  102.3 20.7 %collective-permute-start.26 = (f32[256]{0:T(256)S(1)}, f32[256]{0:T(256)S(1)}, u32[]{:S(2)}, u32[]{:S(2)}) collective-permute-start(f32[256]{0:T(256)S(1)} %reshape_squeeze.3), channel_id=1, source_target_pairs={{1,0},{2,1},{3,2},{4,3},{5,4},{6,5},{7,6},{8,7},{9,8},{10,9},{11,1... | collective-permute-start | bytes 3080 | tf_op jit(solution)/shard_map/ppermute | solution.py:37
  111.1 11.9 %collective-permute-start.27 = (f32[256]{0:T(256)S(1)}, f32[256]{0:T(256)S(1)}, u32[]{:S(2)}, u32[]{:S(2)}) collective-permute-start(f32[256]{0:T(256)S(1)} %reshape_squeeze.3), channel_id=1, source_target_pairs={{2,0},{3,1},{4,2},{5,3},{6,4},{7,5},{8,6},{9,7},{10,8},{11,9},{12,... | collective-permute-start | bytes 3080 | tf_op jit(solution)/shard_map/ppermute | solution.py:37
  115.5 7.6 %collective-permute-start.22 = (f32[2,66,1]{2,1,0:T(8,128)S(1)}, f32[2,66,1]{2,1,0:T(8,128)S(1)}, u32[]{:S(2)}, u32[]{:S(2)}) collective-permute-start(f32[2,66,1]{2,1,0:T(8,128)S(1)} %get-tuple-element.63), channel_id=1, source_target_pairs={{512,0},{513,1},{514,2},{515,3},{516,4},{517,5},{518,6},{519,7},{5... | collective-permute-start | bytes 1592 | tf_op jit(solution)/shard_map/ppermute | solution.py:27
  121.6 3.2 %collective-permute-start.23 = (f32[2,66,1]{2,1,0:T(8,128)S(1)}, f32[2,66,1]{2,1,0:T(8,128)S(1)}, u32[]{:S(2)}, u32[]{:S(2)}) collective-permute-start(f32[2,66,1]{2,1,0:T(8,128)S(1)} %get-tuple-element.64), channel_id=1, source_target_pairs={{0,512},{1,513},{2,514},{3,515},{4,516},{5,517},{6,518},{7,519},{8... | collective-permute-start | bytes 1592 | tf_op jit(solution)/shard_map/ppermute | solution.py:25
  125.9 5.3 %collective-permute-start.28 = (f32[1,256]{1,0:T(1,128)S(1)}, f32[1,256]{1,0:T(1,128)S(1)}, u32[]{:S(2)}, u32[]{:S(2)}) collective-permute-start(f32[1,256]{1,0:T(1,128)S(1)} %get-tuple-element.74), channel_id=1, source_target_pairs={{1,0},{2,1},{3,2},{4,3},{5,4},{6,5},{7,6},{8,7},{9,8},{10,9},{11,1... | collective-permute-start | bytes 3080 | tf_op jit(solution)/shard_map/ppermute | solution.py:27
  127.8 9.7 %collective-permute-start.29 = (f32[1,256]{1,0:T(1,128)S(1)}, f32[1,256]{1,0:T(1,128)S(1)}, u32[]{:S(2)}, u32[]{:S(2)}) collective-permute-start(f32[1,256]{1,0:T(1,128)S(1)} %get-tuple-element.73), channel_id=1, source_target_pairs={{0,1},{1,2},{2,3},{3,4},{4,5},{5,6},{6,7},{7,8},{8,9},{9,10},{10,1... | collective-permute-start | bytes 3080 | tf_op jit(solution)/shard_map/ppermute | solution.py:25
  137.7 8.6 %collective-permute-start.30 = (f32[66,1]{1,0:T(8,128)S(1)}, f32[66,1]{1,0:T(8,128)S(1)}, u32[]{:S(2)}, u32[]{:S(2)}) collective-permute-start(f32[66,1]{1,0:T(8,128)S(1)} %get-tuple-element.69), channel_id=1, source_target_pairs={{512,0},{513,1},{514,2},{515,3},{516,4},{517,5},{518,6},{519,7},{5... | collective-permute-start | bytes 800 | tf_op jit(solution)/shard_map/ppermute | solution.py:27
  144.0 3.1 %collective-permute-start.31 = (f32[66,1]{1,0:T(8,128)S(1)}, f32[66,1]{1,0:T(8,128)S(1)}, u32[]{:S(2)}, u32[]{:S(2)}) collective-permute-start(f32[66,1]{1,0:T(8,128)S(1)} %get-tuple-element.70), channel_id=1, source_target_pairs={{0,512},{1,513},{2,514},{3,515},{4,516},{5,517},{6,518},{7,519},{8... | collective-permute-start | bytes 800 | tf_op jit(solution)/shard_map/ppermute | solution.py:25
  147.3 5.3 %collective-permute-start.32 = (f32[2,1,256]{2,1,0:T(1,128)S(1)}, f32[2,1,256]{2,1,0:T(1,128)S(1)}, u32[]{:S(2)}, u32[]{:S(2)}) collective-permute-start(f32[2,1,256]{2,1,0:T(1,128)S(1)} %get-tuple-element.66), channel_id=1, source_target_pairs={{1,0},{2,1},{3,2},{4,3},{5,4},{6,5},{7,6},{8,7},{9,8},{10,9},{11,1... | collective-permute-start | bytes 6152 | tf_op jit(solution)/shard_map/ppermute | solution.py:27
  149.2 9.8 %collective-permute-start.33 = (f32[2,1,256]{2,1,0:T(1,128)S(1)}, f32[2,1,256]{2,1,0:T(1,128)S(1)}, u32[]{:S(2)}, u32[]{:S(2)}) collective-permute-start(f32[2,1,256]{2,1,0:T(1,128)S(1)} %get-tuple-element.65), channel_id=1, source_target_pairs={{0,1},{1,2},{2,3},{3,4},{4,5},{5,6},{6,7},{7,8},{8,9},{9,10},{10,1... | collective-permute-start | bytes 6152 | tf_op jit(solution)/shard_map/ppermute | solution.py:25
  159.0 15.6 %collective-permute-start.34 = (f32[2,66,1]{2,1,0:T(8,128)S(1)}, f32[2,66,1]{2,1,0:T(8,128)S(1)}, u32[]{:S(2)}, u32[]{:S(2)}) collective-permute-start(f32[2,66,1]{2,1,0:T(8,128)S(1)} %get-tuple-element.61), channel_id=1, source_target_pairs={{512,0},{513,1},{514,2},{515,3},{516,4},{517,5},{518,6},{519,7},{5... | collective-permute-start | bytes 1592 | tf_op jit(solution)/shard_map/ppermute | solution.py:27
  162.4 12.3 %collective-permute-start.35 = (f32[2,66,1]{2,1,0:T(8,128)S(1)}, f32[2,66,1]{2,1,0:T(8,128)S(1)}, u32[]{:S(2)}, u32[]{:S(2)}) collective-permute-start(f32[2,66,1]{2,1,0:T(8,128)S(1)} %get-tuple-element.62), channel_id=1, source_target_pairs={{0,512},{1,513},{2,514},{3,515},{4,516},{5,517},{6,518},{7,519},{8... | collective-permute-start | bytes 1592 | tf_op jit(solution)/shard_map/ppermute | solution.py:25
  163.7 12.6 %collective-permute-start.12 = (f32[3,2,64,128]{3,2,1,0:T(8,128)S(1)}, f32[3,2,64,128]{3,2,1,0:T(8,128)S(1)}, u32[]{:S(2)}, u32[]{:S(2)}) collective-permute-start(f32[3,2,64,128]{3,2,1,0:T(8,128)S(1)} %get-tuple-element.55), channel_id=1, source_target_pairs={{0,1},{1,2},{2,3},{3,4},{4,5},{5,6},{6,7},{7,8},{8,9},{9,10},{10,1... | collective-permute-start | bytes 589832 | tf_op jit(solution)/shard_map/ppermute | solution.py:25
  165.6 11.4 %collective-permute-start.13 = (f32[3,2,64,128]{3,2,1,0:T(8,128)S(1)}, f32[3,2,64,128]{3,2,1,0:T(8,128)S(1)}, u32[]{:S(2)}, u32[]{:S(2)}) collective-permute-start(f32[3,2,64,128]{3,2,1,0:T(8,128)S(1)} %get-tuple-element.56), channel_id=1, source_target_pairs={{1,0},{2,1},{3,2},{4,3},{5,4},{6,5},{7,6},{8,7},{9,8},{10,9},{11,1... | collective-permute-start | bytes 589832 | tf_op jit(solution)/shard_map/ppermute | solution.py:27
  177.0 6.4 %collective-permute-start.14 = (f32[3,8,2,128]{3,2,1,0:T(2,128)S(1)}, f32[3,8,2,128]{3,2,1,0:T(2,128)S(1)}, u32[]{:S(2)}, u32[]{:S(2)}) collective-permute-start(f32[3,8,2,128]{3,2,1,0:T(2,128)S(1)} %get-tuple-element.46), channel_id=1, source_target_pairs={{0,512},{1,513},{2,514},{3,515},{4,516},{5,517},{6,518},{7,519},{8... | collective-permute-start | bytes 73736 | tf_op jit(solution)/shard_map/ppermute | solution.py:25
  178.3 5.2 %collective-permute-start.15 = (f32[3,8,2,128]{3,2,1,0:T(2,128)S(1)}, f32[3,8,2,128]{3,2,1,0:T(2,128)S(1)}, u32[]{:S(2)}, u32[]{:S(2)}) collective-permute-start(f32[3,8,2,128]{3,2,1,0:T(2,128)S(1)} %get-tuple-element.47), channel_id=1, source_target_pairs={{512,0},{513,1},{514,2},{515,3},{516,4},{517,5},{518,6},{519,7},{5... | collective-permute-start | bytes 73736 | tf_op jit(solution)/shard_map/ppermute | solution.py:27
  184.2 0.9 copy-start.7
  184.2 1.0 copy-start.8
  186.8 0.9 copy-start.12
where the time goes:
time: 189 us; the launch traced here: 188 us
  starting transfers between devices  137 us (72%)
  waiting for transfers between devices  26.6 us (14%)
  other arithmetic  14.7 us (8%)
  local copies, waits for them, and re-layouts  6.87 us (4%)
    ppermute x16, starting transfers between devices, extended(): lax.ppermute(head, axis, [((i + 1) % count, i) for i in range(ends)])  89.9 us
    ppermute x16, starting transfers between devices, extended(): lax.ppermute(tail, axis, [(i, (i + 1) % count) for i in range(ends)])  30.1 us
    ppermute x16, waiting for transfers between devices, extended(): lax.ppermute(tail, axis, [(i, (i + 1) % count) for i in range(ends)])  22.7 us
    ppermute x4, starting transfers between devices, from_behind(): lax.ppermute(value, axis, [(source, source + steps) for source in range(l...  16.9 us
    concatenate x8, other arithmetic, extended(): jnp.concatenate([lax.ppermute(tail, axis, [(i, (i + 1) % count) for i in...  4.76 us
    ppermute x16, waiting for transfers between devices, extended(): lax.ppermute(head, axis, [((i + 1) % count, i) for i in range(ends)])  3.9 us
  transfers between devices with their start and end apart: 36, of which 14 were waited for; matrix products, arithmetic and copies ran while one was open for 5% of the time, Pallas kernels for 0%

commit v1 on v0

v1 whole, which is shorter than its diff:
```python
import functools

import jax
import jax.numpy as jnp
from jax import lax
from jax.experimental import pallas as pl
from jax.experimental.pallas import tpu as pltpu
from jax.sharding import PartitionSpec as P

REACH = 2
FAR_REACH = REACH + 1
NEAR_COEF = 9.0 / 8.0
FAR_COEF = -1.0 / 24.0
TIME_STEP = 0.15
OCEAN_STEP = 0.3
MESH = pl.DeviceIdType.MESH

YY, YZ, XY, XZ, XX, ZZ = range(6)
SOURCE = (1, 5, 3, 4, 0, 2)

PAD = 8
LAY = 2


def lane_coefs(shape):
    lane = lax.broadcasted_iota(jnp.int32, shape, len(shape) - 1)
    last = shape[-1] - 1

    def coef(value, keep):
        return jnp.where(keep, jnp.float32(value), jnp.float32(0.0))

    forward = (
        coef(NEAR_COEF, lane < last),
        coef(FAR_COEF, lane < last - 1),
        coef(-FAR_COEF, lane > 0),
    )
    backward = (
        coef(-NEAR_COEF, lane > 0),
        coef(FAR_COEF, lane < last),
        coef(-FAR_COEF, lane > 1),
    )
    return forward, backward


def forward_z(f, coefs):
    n, axis = f.shape[-1], f.ndim - 1
    one, two, back = coefs
    return (
        one * pltpu.roll(f, n - 1, axis)
        - NEAR_COEF * f
        + two * pltpu.roll(f, n - 2, axis)
        + back * pltpu.roll(f, 1, axis)
    )


def backward_z(f, coefs):
    n, axis = f.shape[-1], f.ndim - 1
    back, one, two = coefs
    return (
        NEAR_COEF * f
        + back * pltpu.roll(f, 1, axis)
        + one * pltpu.roll(f, n - 1, axis)
        + two * pltpu.roll(f, 2, axis)
    )


def kernel(
    tiles,
    vel_in, str_in, buo_in, lam_in, mu_in, oce_in, dep_in, wet_in, src_in, share_in,
    vel_out, str_out, oce_out,
    s0, s1, v0, v1, v2, buo, lam, mu,
    src, share, oce, dep, wet, loc, locn, pat, row, flux, vel1,
    load_sem, xs_sem, xr_sem, ys_sem, yr_sem, os_sem, or_sem, ps_sem, pr_sem,
):
    cx, cy, nz = buo_in.shape
    ocx, ocy = dep_in.shape
    half = ocy // 2
    tile = lax.axis_index("tile")
    sec = lax.axis_index("sec")
    has_low = tile > 0
    has_high = tile < tiles - 1
    own = pl.ds(LAY, cx)
    rows_own = pl.ds(PAD, cy)
    orow_own = pl.ds(PAD, ocx)

    def device(step, other=False):
        return {"sec": 1 - sec if other else sec, "tile": tile + step}

    loads = [
        pltpu.make_async_copy(str_in.at[SOURCE[c]], s0.at[c, own, rows_own], load_sem.at[c])
        for c in range(6)
    ]
    loads += [
        pltpu.make_async_copy(vel_in, v0, load_sem.at[6]),
        pltpu.make_async_copy(buo_in, buo, load_sem.at[7]),
        pltpu.make_async_copy(lam_in, lam, load_sem.at[8]),
        pltpu.make_async_copy(mu_in, mu, load_sem.at[9]),
    ]
    ocean_loads = [
        pltpu.make_async_copy(oce_in, oce.at[:, orow_own, 0:ocy], load_sem.at[10]),
        pltpu.make_async_copy(dep_in, dep.at[orow_own, 0:ocy], load_sem.at[11]),
        pltpu.make_async_copy(wet_in, wet.at[orow_own, 0:ocy], load_sem.at[12]),
    ]
    row_loads = [
        pltpu.make_async_copy(src_in, src, load_sem.at[13]),
        pltpu.make_async_copy(share_in, share, load_sem.at[14]),
    ]
    for copy in row_loads + loads + ocean_loads:
        copy.start()

    outer = pl.multiple_of((cy + PAD) * sec, 8)
    for field in (s0, s1):
        field[0:3, own, pl.ds(outer, PAD), :] = jnp.zeros((3, cx, PAD, nz), jnp.float32)
    for field in (v1, v2):
        field[:, own, pl.ds(outer, PAD), :] = jnp.zeros((3, cx, PAD, nz), jnp.float32)
    pat[...] = jnp.zeros(pat.shape, jnp.float32)

    def clear(layers, orow, slot):
        for field in (s0, s1):
            field[XY : XX + 1, layers, rows_own, :] = jnp.zeros((3, LAY, cy, nz), jnp.float32)
        for field in (v1, v2):
            field[:, layers, rows_own, :] = jnp.zeros((3, LAY, cy, nz), jnp.float32)
        oce[:, orow, 0:ocy] = jnp.zeros((3, PAD, ocy), jnp.float32)
        dep[orow, 0:ocy] = jnp.zeros((PAD, ocy), jnp.float32)
        wet[orow, 0:ocy] = jnp.zeros((PAD, ocy), jnp.int32)
        locn[slot] = jnp.zeros(locn.shape[1:], jnp.float32)

    @pl.when(jnp.logical_not(has_low))
    def _():
        clear(slice(0, LAY), slice(0, PAD), 0)

    @pl.when(jnp.logical_not(has_high))
    def _():
        clear(slice(LAY + cx, LAY + cx + LAY), slice(PAD + ocx, PAD + ocx + PAD), 1)

    barrier = pltpu.get_barrier_semaphore()
    pl.semaphore_signal(barrier, inc=1, device_id=device(0, True), device_id_type=MESH)

    @pl.when(has_low)
    def _():
        pl.semaphore_signal(barrier, inc=1, device_id=device(-1), device_id_type=MESH)

    @pl.when(has_high)
    def _():
        pl.semaphore_signal(barrier, inc=1, device_id=device(1), device_id_type=MESH)

    pl.semaphore_wait(barrier, 1 + has_low.astype(jnp.int32) + has_high.astype(jnp.int32))

    def copy_to(source, target, send, receive, where):
        return pltpu.make_async_remote_copy(
            src_ref=source, dst_ref=target, send_sem=send, recv_sem=receive,
            device_id=where, device_id_type=MESH,
        )

    low, high = LAY, LAY + cx

    def x_copies(number, field, source=None):
        up, down = [], []
        if number % 2 == 0:
            if source is None:
                near = field.at[XX, :, rows_own]
                far = field.at[XY : XZ + 1, :, rows_own]
                shift = 0
            else:
                near = source.at[SOURCE[XX]]
                far = source.at[SOURCE[XY] : SOURCE[XZ] + 1]
                shift = LAY
            ups = [
                (near.at[high - 1 - shift : high - shift], field.at[XX, 1:2, rows_own]),
                (far.at[:, high - 2 - shift : high - shift], field.at[XY : XZ + 1, 0:2, rows_own]),
            ]
            downs = [
                (near.at[low - shift : low + 2 - shift], field.at[XX, high : high + 2, rows_own]),
                (far.at[:, low - shift : low + 1 - shift], field.at[XY : XZ + 1, high : high + 1, rows_own]),
            ]
        else:
            near = field.at[0, :, rows_own]
            far = field.at[1:3, :, rows_own]
            ups = [
                (near.at[high - 2 : high], field.at[0, 0:2, rows_own]),
                (far.at[:, high - 1 : high], field.at[1:3, 1:2, rows_own]),
            ]
            downs = [
                (near.at[low : low + 1], field.at[0, high : high + 1, rows_own]),
                (far.at[:, low : low + 2], field.at[1:3, high : high + 2, rows_own]),
            ]
        for i, (a, b) in enumerate(ups):
            up.append(copy_to(a, b, xs_sem.at[number, 0, i], xr_sem.at[number, 0, i], device(1)))
        for i, (a, b) in enumerate(downs):
            down.append(copy_to(a, b, xs_sem.at[number, 1, i], xr_sem.at[number, 1, i], device(-1)))
        return up, down

    def start(copies):
        up, down = copies

        @pl.when(has_high)
        def _():
            for copy in up:
                copy.start()

        @pl.when(has_low)
        def _():
            for copy in down:
                copy.start()

    def arrive(copies):
        up, down = copies

        @pl.when(has_low)
        def _():
            for copy in up:
                copy.wait_recv()

        @pl.when(has_high)
        def _():
            for copy in down:
                copy.wait_recv()

    def sent(copies):
        up, down = copies

        @pl.when(has_high)
        def _():
            for copy in up:
                copy.wait_send()

        @pl.when(has_low)
        def _():
            for copy in down:
                copy.wait_send()

    y_from = pl.multiple_of(cy - (cy - PAD) * sec, 8)
    y_to = pl.multiple_of((cy + PAD) * sec, 8)

    def y_copy(number, field):
        part = field.at[0:3, own]
        return copy_to(
            part.at[:, :, pl.ds(y_from, PAD)],
            part.at[:, :, pl.ds(y_to, PAD)],
            ys_sem.at[number], yr_sem.at[number], device(0, True),
        )

    x_s0 = x_copies(0, s0, str_in)
    start(x_s0)

    loc[...] = jnp.zeros(loc.shape, jnp.float32)
    for copy in row_loads:
        copy.wait()
    loc[0:1, 0:ocx] = src[...].astype(jnp.float32)
    loc[1:2, 0:ocx] = share[...]

    def ocean_rows(step, first, target, slot, index):
        return [
            copy_to(oce_in.at[:, pl.ds(first, PAD)], oce.at[:, pl.ds(target, PAD), 0:ocy], os_sem.at[index, 0], or_sem.at[index, 0], device(step)),
            copy_to(dep_in.at[pl.ds(first, PAD)], dep.at[pl.ds(target, PAD), 0:ocy], os_sem.at[index, 1], or_sem.at[index, 1], device(step)),
            copy_to(wet_in.at[pl.ds(first, PAD)], wet.at[pl.ds(target, PAD), 0:ocy], os_sem.at[index, 2], or_sem.at[index, 2], device(step)),
            copy_to(loc, locn.at[slot], os_sem.at[index, 3], or_sem.at[index, 3], device(step)),
        ]

    x_ocean = (
        ocean_rows(1, ocx - PAD, 0, 0, 0),
        ocean_rows(-1, 0, PAD + ocx, 1, 1),
    )
    start(x_ocean)

    for copy in loads:
        copy.wait()
    y_s0 = y_copy(0, s0)
    y_s0.start()

    forward, backward = lane_coefs((1, 1, nz))

    def forward_x(a):
        return NEAR_COEF * (a[2 : 2 + cx] - a[1 : 1 + cx]) + FAR_COEF * (a[3 : 3 + cx] - a[0:cx])

    def backward_x(a):
        return NEAR_COEF * (a[2 : 2 + cx] - a[1 : 1 + cx]) + FAR_COEF * (a[3 : 3 + cx] - a[0:cx])

    def velocity_rows(i, old, stress, new, out=None):
        base = pl.multiple_of(PAD + i * 8, 8)
        here = pl.ds(pl.multiple_of(i * 8, 8), 8)

        def at(c, layers, shift=0):
            return stress[c, layers, pl.ds(base + shift, 8), :]

        def fy(c):
            return NEAR_COEF * (at(c, own, 1) - at(c, own)) + FAR_COEF * (at(c, own, 2) - at(c, own, -1))

        def by(c):
            return NEAR_COEF * (at(c, own) - at(c, own, -1)) + FAR_COEF * (at(c, own, 1) - at(c, own, -2))

        def fx(c):
            return forward_x(at(c, pl.ds(LAY - 1, cx + 3)))

        def bx(c):
            return backward_x(at(c, pl.ds(LAY - 2, cx + 3)))

        scale = TIME_STEP * buo[:, here, :]
        x = fx(XX) + by(XY) + backward_z(at(XZ, own), backward)
        y = bx(XY) + fy(YY) + backward_z(at(YZ, own), backward)
        z = bx(XZ) + by(YZ) + forward_z(at(ZZ, own), forward)
        if old is v0:
            before = old[:, :, here, :]
        else:
            before = old[:, own, pl.ds(base, 8), :]
        for c, value in enumerate((x, y, z)):
            result = before[c] + scale * value
            new[c, own, pl.ds(base, 8), :] = result
            if out is not None:
                out[c, :, here, :] = result

    def stress_rows(i, old, velocity, new, last):
        base = pl.multiple_of(PAD + i * 8, 8)
        here = pl.ds(pl.multiple_of(i * 8, 8), 8)

        def at(c, layers, shift=0):
            return velocity[c, layers, pl.ds(base + shift, 8), :]

        def fy(c):
            return NEAR_COEF * (at(c, own, 1) - at(c, own)) + FAR_COEF * (at(c, own, 2) - at(c, own, -1))

        def by(c):
            return NEAR_COEF * (at(c, own) - at(c, own, -1)) + FAR_COEF * (at(c, own, 1) - at(c, own, -2))

        def fx(c):
            return forward_x(at(c, pl.ds(LAY - 1, cx + 3)))

        strain_x = backward_x(at(0, pl.ds(LAY - 2, cx + 3)))
        strain_y = by(1)
        strain_z = backward_z(at(2, own), backward)
        shear = TIME_STEP * mu[:, here, :]
        volume = TIME_STEP * lam[:, here, :] * (strain_x + strain_y + strain_z)
        change = {
            XX: volume + 2.0 * shear * strain_x,
            YY: volume + 2.0 * shear * strain_y,
            ZZ: volume + 2.0 * shear * strain_z,
            XY: shear * (fy(0) + fx(1)),
            XZ: shear * (forward_z(at(0, own), forward) + fx(2)),
            YZ: shear * (forward_z(at(1, own), forward) + fy(2)),
        }
        for c, value in change.items():
            result = old[c, own, pl.ds(base, 8), :] + value
            if last:
                new[SOURCE[c], :, here, :] = result
            else:
                new[c, own, pl.ds(base, 8), :] = result

    def each(function, *args):
        def body(i, carry):
            function(i, *args)
            return carry

        lax.fori_loop(0, cy // 8, body, 0)

    y_s0.wait_recv()
    arrive(x_s0)
    each(velocity_rows, v0, s0, v1)
    x_v1, y_v1 = x_copies(1, v1), y_copy(1, v1)
    start(x_v1)
    y_v1.start()

    for copy in ocean_loads:
        copy.wait()
    arrive(x_ocean)
    edge = pl.multiple_of(half * (1 - sec), 128)

    def ocean_columns(field, index):
        part = field.at[:, :, :] if len(field.shape) == 3 else field.at[:, :]
        if len(field.shape) == 3:
            a, b = part.at[:, :, pl.ds(edge, half)], part.at[:, :, ocy : ocy + half]
        else:
            a, b = part.at[:, pl.ds(edge, half)], part.at[:, ocy : ocy + half]
        return copy_to(a, b, os_sem.at[2, index], or_sem.at[2, index], device(0, True))

    y_ocean = [ocean_columns(oce, 0), ocean_columns(dep, 1), ocean_columns(wet, 2)]
    for copy in y_ocean:
        copy.start()

    lane = lax.broadcasted_iota(jnp.int32, (8, 128), 1)

    def spread(value):
        return jnp.broadcast_to(value, (8, 128))

    def lanes_of(index):
        mine = pltpu.roll(spread(loc[index : index + 1, :]), PAD, 1)
        below = pltpu.roll(spread(locn[0, index : index + 1, :]), 128 - (ocx - PAD), 1)
        above = pltpu.roll(spread(locn[1, index : index + 1, :]), PAD + ocx, 1)
        return jnp.where(lane < PAD, below, jnp.where(lane < PAD + ocx, mine, above))

    slot = lax.broadcasted_iota(jnp.int32, (8, 128), 0)
    picked = lanes_of(0).astype(jnp.int32) - tile + FAR_REACH == slot
    row[...] = jnp.where(picked, OCEAN_STEP * lanes_of(1), 0.0)

    y_v1.wait_recv()
    arrive(x_v1)
    each(stress_rows, s0, v1, s1, False)
    x_s1, y_s1 = x_copies(2, s1), y_copy(2, s1)
    start(x_s1)
    y_s1.start()

    for copy in y_ocean:
        copy.wait()
    region = oce.shape[1:]
    width = region[1]
    lanes = lax.broadcasted_iota(jnp.int32, (1, width), 1)
    beyond = lanes - ocy
    inside = (beyond < 0) | ((beyond < half // 2) & (sec == 0)) | ((beyond >= half // 2) & (sec == 1))
    rows = lax.broadcasted_iota(jnp.int32, (region[0], 1), 0)
    inside_rows = ((rows >= PAD) | has_low) & ((rows < PAD + ocx) | has_high)
    mask = inside.astype(jnp.float32) * inside_rows.astype(jnp.float32)
    wetf = wet[...].astype(jnp.float32) * mask
    vel1[3] = wetf
    oce[0] = oce[0] * mask
    HALF_STEP = 0.5 * OCEAN_STEP

    def ocean_flow(eta, u, v, first, count, out_u, out_v):
        here = pl.ds(first, count)
        middle = eta[here, :]
        w = vel1[3, here, :]
        new_u = w * (u[here, :] - HALF_STEP * (eta[pl.ds(first + 1, count), :] - eta[pl.ds(first - 1, count), :]))
        new_v = w * (v[here, :] - HALF_STEP * (pltpu.roll(middle, width - 1, 1) - pltpu.roll(middle, 1, 1)))
        out_u[here, :] = new_u
        out_v[here, :] = new_v
        flux[0, here, :] = dep[here, :] * new_u
        flux[1, here, :] = dep[here, :] * new_v

    def ocean_fall(first, count):
        along = flux[1, pl.ds(first, count), :]
        return HALF_STEP * (
            flux[0, pl.ds(first + 1, count), :] - flux[0, pl.ds(first - 1, count), :]
            + pltpu.roll(along, width - 1, 1) - pltpu.roll(along, 1, 1)
        )

    ocean_flow(oce.at[0], oce.at[1], oce.at[2], 4, ocx + 8, vel1.at[0], vel1.at[1])
    here = pl.ds(5, ocx + 6)
    rows_here = lax.broadcasted_iota(jnp.int32, (ocx + 6, 1), 0) + 5
    mask_here = inside.astype(jnp.float32) * (
        ((rows_here >= PAD) | has_low) & ((rows_here < PAD + ocx) | has_high)
    ).astype(jnp.float32)
    vel1[2, here, :] = (oce[0, here, :] - ocean_fall(5, ocx + 6)) * mask_here

    y_s1.wait_recv()
    arrive(x_s1)
    each(velocity_rows, v1, s1, v2, vel_out)
    x_v2, y_v2 = x_copies(3, v2), y_copy(3, v2)
    start(x_v2)
    y_v2.start()

    top = v2[2, own, rows_own, :].reshape(cx * cy, nz)
    first_lane = (lax.broadcasted_iota(jnp.int32, (8, nz), 1) == 0).astype(jnp.float32)
    patch = lax.dot_general(
        first_lane, top, (((1,), (1,)), ((), ())),
        precision=lax.Precision.HIGHEST, preferred_element_type=jnp.float32,
    )
    pat[8:16, 0:ocy] = patch
    patch_copies = []
    for other in (False, True):
        for step in range(-FAR_REACH, FAR_REACH + 1):
            if step == 0 and not other:
                continue
            index = FAR_REACH - step
            if other:
                source = pat.at[8:9, pl.ds(edge, half)]
                target = pat.at[index : index + 1, ocy : ocy + half]
            else:
                source = pat.at[8:9, 0:ocy]
                target = pat.at[index : index + 1, 0:ocy]
            copy = copy_to(source, target, ps_sem.at[int(other), index], pr_sem.at[int(other), index], device(step, other))
            back = (tile - step >= 0) & (tile - step < tiles)
            ahead = (tile + step >= 0) & (tile + step < tiles)
            patch_copies.append((copy, ahead, back))
    for copy, ahead, back in patch_copies:
        pl.when(ahead)(copy.start)
    pat[FAR_REACH : FAR_REACH + 1, 0:ocy] = patch[0:1]

    y_v2.wait_recv()
    arrive(x_v2)
    each(stress_rows, s1, v2, str_out, True)

    for copy, ahead, back in patch_copies:
        pl.when(back)(copy.wait_recv)
    uplift = lax.dot_general(
        row[...], pat[0:8, :], (((0,), (0,)), ((), ())),
        precision=lax.Precision.HIGHEST, preferred_element_type=jnp.float32,
    )[0 : PAD + ocx + PAD]
    source = vel1[3] * uplift
    oce[0] = vel1[2] + source
    ocean_flow(oce.at[0], vel1.at[0], vel1.at[1], PAD - 1, ocx + 2, oce.at[1], oce.at[2])
    oce_out[0] = oce[0, orow_own, 0:ocy] - ocean_fall(PAD, ocx)[:, 0:ocy] + source[PAD : PAD + ocx, 0:ocy]
    oce_out[1:3] = oce[1:3, orow_own, 0:ocy]

    for copies in (x_s0, x_ocean, x_v1, x_s1, x_v2):
        sent(copies)
    for copy in (y_s0, y_v1, y_s1, y_v2):
        copy.wait_send()
    for copy, ahead, back in patch_copies:
        pl.when(ahead)(copy.wait_send)


def solution(mesh):
    tiles = mesh.shape["tile"]

    def shards(velocity, stresses, buoyancy, lame_first, shear_mod, ocean_state, depth_map, wet_mask, src, share):
        cx, cy, nz = buoyancy.shape
        ocx, ocy = depth_map.shape
        layers, rows = cx + 2 * LAY, cy + 2 * PAD
        region = (ocx + 2 * PAD, ocy + ocy // 2)
        hbm = pl.BlockSpec(memory_space=pltpu.HBM)
        vmem = pl.BlockSpec(memory_space=pltpu.VMEM)
        dma = pltpu.SemaphoreType.DMA
        f32 = jnp.float32
        return pl.pallas_call(
            functools.partial(kernel, tiles),
            out_shape=(
                jax.ShapeDtypeStruct(velocity.shape, f32),
                jax.ShapeDtypeStruct(stresses.shape, f32),
                jax.ShapeDtypeStruct(ocean_state.shape, f32),
            ),
            in_specs=[hbm] * 10,
            out_specs=(vmem,) * 3,
            scratch_shapes=[
                pltpu.VMEM((6, layers, rows, nz), f32),
                pltpu.VMEM((6, layers, rows, nz), f32),
                pltpu.VMEM(velocity.shape, f32),
                pltpu.VMEM((3, layers, rows, nz), f32),
                pltpu.VMEM((3, layers, rows, nz), f32),
                pltpu.VMEM(buoyancy.shape, f32),
                pltpu.VMEM(buoyancy.shape, f32),
                pltpu.VMEM(buoyancy.shape, f32),
                pltpu.VMEM((1, ocx), jnp.int32),
                pltpu.VMEM((1, ocx), f32),
                pltpu.VMEM((3, *region), f32),
                pltpu.VMEM(region, f32),
                pltpu.VMEM(region, jnp.int32),
                pltpu.VMEM((8, 128), f32),
                pltpu.VMEM((2, 8, 128), f32),
                pltpu.VMEM((16, region[1]), f32),
                pltpu.VMEM((8, 128), f32),
                pltpu.VMEM((2, *region), f32),
                pltpu.VMEM((4, *region), f32),
                dma((15,)),
                dma((4, 2, 2)),
                dma((4, 2, 2)),
                dma((4,)),
                dma((4,)),
                dma((3, 4)),
                dma((3, 4)),
                dma((2, 7)),
                dma((2, 7)),
            ],
            compiler_params=pltpu.CompilerParams(
                collective_id=0, has_side_effects=True, vmem_limit_bytes=40 * 1024 * 1024
            ),
        )(
            *(
                pltpu.with_memory_space_constraint(array, pltpu.HBM)
                for array in (
                    velocity, stresses, buoyancy, lame_first, shear_mod, ocean_state, depth_map, wet_mask,
                    src.reshape(1, ocx), share.reshape(1, ocx),
                )
            )
        )

    return jax.shard_map(
        shards,
        mesh=mesh,
        in_specs=(
            P(None, "tile", "sec", None),
            P(None, "tile", "sec", None),
            P("tile", "sec", None),
            P("tile", "sec", None),
            P("tile", "sec", None),
            P(None, "tile", "sec"),
            P("tile", "sec"),
            P("tile", "sec"),
            P("tile"),
            P("tile"),
        ),
        out_specs=(
            P(None, "tile", "sec", None),
            P(None, "tile", "sec", None),
            P(None, "tile", "sec"),
        ),
        check_vma=False,
    )
```

time: 189 us -> 56 us (0.30)
  starting transfers between devices: 137 us -> 0 us
  Pallas kernels: 0 us -> 52.2 us
  waiting for transfers between devices: 26.6 us -> 0 us
  other arithmetic: 14.7 us -> 0 us
  local copies, waits for them, and re-layouts: 6.87 us -> 2.3 us
    ppermute x36 -> x0, starting transfers between devices: 137 us -> none  [the longest x16 89.9 us: extended(): lax.ppermute(head, axis, [((i + 1) % count, i) for i in range(ends)])]
    pallas_call x0 -> x1, Pallas kernels: none -> 52.2 us  [shards(): pl.pallas_call(functools.partial(kernel, tiles), out_shape=(jax.ShapeDtyp...]
    ppermute x36 -> x0, waiting for transfers between devices: 26.6 us -> none  [the longest x16 22.7 us: extended(): lax.ppermute(tail, axis, [(i, (i + 1) % count) for i in range(ends)])]
    another operation x15 -> x0, other arithmetic: 6.04 us -> none  [the longest x6 2.74 us: update_velocity(): jnp.stack([accel_x, accel_y, accel_z])]
    concatenate x8 -> x0, other arithmetic: 4.76 us -> none  [extended(): jnp.concatenate([lax.ppermute(tail, axis, [(i, (i + 1) % count) for i in...]
    unnamed x10 -> x0, other arithmetic: 3.11 us -> none
    slice x12 -> x0, local copies, waits for them, and re-layouts: 2.55 us -> none  [the longest x5 1.57 us: extended(): head = lax.slice_in_dim(cells, 0, width, axis=dim)]
  transfers between devices with their start and end apart: 36 -> 0, of which waited for: 14 -> 0; matrix products, arithmetic and copies ran while one was open for 5% -> 0% of each run, Pallas kernels for 0% -> 0%
where the time goes in v1:
time: 56 us; the launch traced here: 55.2 us
  Pallas kernels  52.2 us (93%)
  local copies, waits for them, and re-layouts  2.3 us (4%)
  between operations  0.64 us (1%)
    pallas_call x1, Pallas kernels, shards(): pl.pallas_call(functools.partial(kernel, tiles), out_shape=(jax.ShapeDtyp...  52.2 us
    unnamed x3, local copies, waits for them, and re-layouts  2.3 us

profile of v1, /device:TPU:9, one launch (start us, length us, event | category | flops | bytes accessed | tf_op | source)
XLA Modules:
  0.0 55.2 jit_solution(6529469818909790660)
XLA Ops:
  0.6 52.2 %shard_map.121 = (f32[3,4,64,128]{3,2,1,0:T(8,128)S(1)}, f32[6,4,64,128]{3,2,1,0:T(8,128)S(1)}, f32[3,64,256]{2,1,0:T(8,128)S(1)}) custom-call(f32[3,4,64,128]{3,2,1,0:T(8,128)} %vel_in.1, f32[6,4,64,128]{3,2,1,0:T(8,128)} %str_in.1, f32[4,64,128]{2,1,0:T(8,128)} %buo_in.1, f32[4,64,128]{2,1,0:T(8,128)} %lam_in.1, f32[4,64,128]{2,1,0:T(8,128)} %mu_in.1, ...), custom_call_target="tpu_custom_call" | custom-call | tf_op jit(solution)/shard_map/pallas_call | solution.py:512
  52.8 0.7 %copy.16 = f32[3,4,64,128]{3,2,1,0:T(8,128)} copy(f32[3,4,64,128]{3,2,1,0:T(8,128)S(1)} %get-tuple-element.6) | data formatting | bytes 786432
  53.6 0.9 %copy.17 = f32[6,4,64,128]{3,2,1,0:T(8,128)} copy(f32[6,4,64,128]{3,2,1,0:T(8,128)S(1)} %get-tuple-element.7) | data formatting | bytes 1572864
  54.5 0.7 %copy.18 = f32[3,64,256]{2,1,0:T(8,128)} copy(f32[3,64,256]{2,1,0:T(8,128)S(1)} %get-tuple-element.8) | data formatting | bytes 393216

commit v2 on v1

--- a/solution.py
+++ b/solution.py
@@ -20,6 +20,7 @@
 
 PAD = 8
 LAY = 2
+BOUNDS = (0, 4, 8)
 
 
 def lane_coefs(shape):
@@ -68,7 +69,7 @@
     tiles,
     vel_in, str_in, buo_in, lam_in, mu_in, oce_in, dep_in, wet_in, src_in, share_in,
     vel_out, str_out, oce_out,
-    s0, s1, v0, v1, v2, buo, lam, mu,
+    s0, sp, s1, v0, v1, v2, buo, lam, mu, stiff,
     src, share, oce, dep, wet, loc, locn, pat, row, flux, vel1,
     load_sem, xs_sem, xr_sem, ys_sem, yr_sem, os_sem, or_sem, ps_sem, pr_sem,
 ):
@@ -94,7 +95,7 @@
         pltpu.make_async_copy(vel_in, v0, load_sem.at[6]),
         pltpu.make_async_copy(buo_in, buo, load_sem.at[7]),
         pltpu.make_async_copy(lam_in, lam, load_sem.at[8]),
-        pltpu.make_async_copy(mu_in, mu, load_sem.at[9]),
+        pltpu.make_async_copy(mu_in, mu.at[own], load_sem.at[9]),
     ]
     ocean_loads = [
         pltpu.make_async_copy(oce_in, oce.at[:, orow_own, 0:ocy], load_sem.at[10]),
@@ -116,10 +117,12 @@
     pat[...] = jnp.zeros(pat.shape, jnp.float32)
 
     def clear(layers, orow, slot):
-        for field in (s0, s1):
+        for field in (s0, sp):
             field[XY : XX + 1, layers, rows_own, :] = jnp.zeros((3, LAY, cy, nz), jnp.float32)
         for field in (v1, v2):
             field[:, layers, rows_own, :] = jnp.zeros((3, LAY, cy, nz), jnp.float32)
+        for field in (mu, stiff):
+            field[layers] = jnp.zeros((LAY, cy, nz), jnp.float32)
         oce[:, orow, 0:ocy] = jnp.zeros((3, PAD, ocy), jnp.float32)
         dep[orow, 0:ocy] = jnp.zeros((PAD, ocy), jnp.float32)
         wet[orow, 0:ocy] = jnp.zeros((PAD, ocy), jnp.int32)
@@ -153,42 +156,69 @@
         )
 
     low, high = LAY, LAY + cx
-
-    def x_copies(number, field, source=None):
-        up, down = [], []
-        if number % 2 == 0:
+    groups = cy // 8
+
+    def bounds_after(bounds):
+        return [0] + [max(b - 1, 0) for b in bounds[1:-1]] + [groups]
+
+    s0_bounds = list(BOUNDS)
+    sp_bounds = bounds_after(s0_bounds)
+    v2_bounds = bounds_after(sp_bounds)
+
+    def rows_of(first, last):
+        return pl.multiple_of(8 * first + sec * (cy - 8 * first - 8 * last), 8), 8 * (last - first)
+
+    S0, V1, SP, V2, STATIC = range(5)
+
+    def x_copies(number, field, chunk=0, first=0, last=groups, source=None):
+        if first == last:
+            return [], []
+        begin, count = rows_of(first, last)
+        rows = pl.ds(PAD + begin, count)
+        if number in (S0, SP):
             if source is None:
-                near = field.at[XX, :, rows_own]
-                far = field.at[XY : XZ + 1, :, rows_own]
+                near, far = field.at[XX, :, rows], field.at[XY : XZ + 1, :, rows]
                 shift = 0
             else:
-                near = source.at[SOURCE[XX]]
-                far = source.at[SOURCE[XY] : SOURCE[XZ] + 1]
+                near = source.at[SOURCE[XX], :, pl.ds(begin, count)]
+                far = source.at[SOURCE[XY] : SOURCE[XZ] + 1, :, pl.ds(begin, count)]
                 shift = LAY
             ups = [
-                (near.at[high - 1 - shift : high - shift], field.at[XX, 1:2, rows_own]),
-                (far.at[:, high - 2 - shift : high - shift], field.at[XY : XZ + 1, 0:2, rows_own]),
+                (near.at[high - 1 - shift : high - shift], field.at[XX, 1:2, rows]),
+                (far.at[:, high - 2 - shift : high - shift], field.at[XY : XZ + 1, 0:2, rows]),
             ]
             downs = [
-                (near.at[low - shift : low + 2 - shift], field.at[XX, high : high + 2, rows_own]),
-                (far.at[:, low - shift : low + 1 - shift], field.at[XY : XZ + 1, high : high + 1, rows_own]),
+                (near.at[low - shift : low + 2 - shift], field.at[XX, high : high + 2, rows]),
+                (far.at[:, low - shift : low + 1 - shift], field.at[XY : XZ + 1, high : high + 1, rows]),
+            ]
+        elif number in (V1, V2):
+            near, far = field.at[0, :, rows], field.at[1:3, :, rows]
+            ups = [
+                (near.at[high - 2 : high], field.at[0, 0:2, rows]),
+                (far.at[:, high - 1 : high], field.at[1:3, 1:2, rows]),
+            ]
+            downs = [
+                (near.at[low : low + 1], field.at[0, high : high + 1, rows]),
+                (far.at[:, low : low + 2], field.at[1:3, high : high + 2, rows]),
             ]
         else:
-            near = field.at[0, :, rows_own]
-            far = field.at[1:3, :, rows_own]
-            ups = [
-                (near.at[high - 2 : high], field.at[0, 0:2, rows_own]),
-                (far.at[:, high - 1 : high], field.at[1:3, 1:2, rows_own]),
-            ]
-            downs = [
-                (near.at[low : low + 1], field.at[0, high : high + 1, rows_own]),
-                (far.at[:, low : low + 2], field.at[1:3, high : high + 2, rows_own]),
-            ]
-        for i, (a, b) in enumerate(ups):
-            up.append(copy_to(a, b, xs_sem.at[number, 0, i], xr_sem.at[number, 0, i], device(1)))
-        for i, (a, b) in enumerate(downs):
-            down.append(copy_to(a, b, xs_sem.at[number, 1, i], xr_sem.at[number, 1, i], device(-1)))
+            ups = [(stiff.at[high - 1 : high], stiff.at[1:2]), (mu.at[high - 2 : high], mu.at[0:2])]
+            downs = [(stiff.at[low : low + 2], stiff.at[high : high + 2]), (mu.at[low : low + 1], mu.at[high : high + 1])]
+        up = [
+            copy_to(a, b, xs_sem.at[number, chunk, 0, i], xr_sem.at[number, chunk, 0, i], device(1))
+            for i, (a, b) in enumerate(ups)
+        ]
+        down = [
+            copy_to(a, b, xs_sem.at[number, chunk, 1, i], xr_sem.at[number, chunk, 1, i], device(-1))
+            for i, (a, b) in enumerate(downs)
+        ]
         return up, down
+
+    def chunks(number, field, bounds, source=None):
+        return [
+            x_copies(number, field, i, first, last, source)
+            for i, (first, last) in enumerate(zip(bounds[:-1], bounds[1:]))
+        ]
 
     def start(copies):
         up, down = copies
@@ -240,8 +270,9 @@
             ys_sem.at[number], yr_sem.at[number], device(0, True),
         )
 
-    x_s0 = x_copies(0, s0, str_in)
-    start(x_s0)
+    x_s0 = chunks(S0, s0, s0_bounds, str_in)
+    for part in x_s0:
+        start(part)
 
     loc[...] = jnp.zeros(loc.shape, jnp.float32)
     for copy in row_loads:
@@ -261,82 +292,89 @@
         ocean_rows(1, ocx - PAD, 0, 0, 0),
         ocean_rows(-1, 0, PAD + ocx, 1, 1),
     )
-    start(x_ocean)
-
     for copy in loads:
         copy.wait()
     y_s0 = y_copy(0, s0)
     y_s0.start()
 
+    buo[...] = TIME_STEP * buo[...]
+    lam[...] = TIME_STEP * lam[...]
+    mu[own] = TIME_STEP * mu[own]
+    stiff[own] = lam[...] + 2.0 * mu[own]
+    x_static = x_copies(STATIC, None)
+    start(x_static)
+    start(x_ocean)
+
     forward, backward = lane_coefs((1, 1, nz))
 
+    def near_far(a, b, c, d):
+        return NEAR_COEF * (a - b) + FAR_COEF * (c - d)
+
+    def outer_x(a):
+        zero = jnp.zeros_like(a[0:1])
+        return jnp.concatenate([zero, zero, a, zero, zero])
+
     def forward_x(a):
-        return NEAR_COEF * (a[2 : 2 + cx] - a[1 : 1 + cx]) + FAR_COEF * (a[3 : 3 + cx] - a[0:cx])
+        return near_far(a[3 : 3 + cx], a[2 : 2 + cx], a[4 : 4 + cx], a[1 : 1 + cx])
 
     def backward_x(a):
-        return NEAR_COEF * (a[2 : 2 + cx] - a[1 : 1 + cx]) + FAR_COEF * (a[3 : 3 + cx] - a[0:cx])
-
-    def velocity_rows(i, old, stress, new, out=None):
-        base = pl.multiple_of(PAD + i * 8, 8)
-        here = pl.ds(pl.multiple_of(i * 8, 8), 8)
-
-        def at(c, layers, shift=0):
+        return near_far(a[2 : 2 + cx], a[1 : 1 + cx], a[3 : 3 + cx], a[0:cx])
+
+    every = pl.ds(0, cx + 2 * LAY)
+
+    def place(g):
+        begin = pl.multiple_of(8 * (g + sec * (groups - 1 - 2 * g)), 8)
+        return pl.ds(begin, 8), begin + PAD
+
+    def velocity_group(g, old, stress, new, halos, out=None):
+        here, base = place(g)
+
+        def at(c, layers=own, shift=0):
             return stress[c, layers, pl.ds(base + shift, 8), :]
 
         def fy(c):
-            return NEAR_COEF * (at(c, own, 1) - at(c, own)) + FAR_COEF * (at(c, own, 2) - at(c, own, -1))
+            return near_far(at(c, own, 1), at(c), at(c, own, 2), at(c, own, -1))
 
         def by(c):
-            return NEAR_COEF * (at(c, own) - at(c, own, -1)) + FAR_COEF * (at(c, own, 1) - at(c, own, -2))
-
-        def fx(c):
-            return forward_x(at(c, pl.ds(LAY - 1, cx + 3)))
-
-        def bx(c):
-            return backward_x(at(c, pl.ds(LAY - 2, cx + 3)))
-
-        scale = TIME_STEP * buo[:, here, :]
-        x = fx(XX) + by(XY) + backward_z(at(XZ, own), backward)
-        y = bx(XY) + fy(YY) + backward_z(at(YZ, own), backward)
-        z = bx(XZ) + by(YZ) + forward_z(at(ZZ, own), forward)
-        if old is v0:
-            before = old[:, :, here, :]
-        else:
-            before = old[:, own, pl.ds(base, 8), :]
+            return near_far(at(c), at(c, own, -1), at(c, own, 1), at(c, own, -2))
+
+        def wide(c):
+            return at(c, every) if halos else outer_x(at(c))
+
+        scale = buo[:, here, :]
+        x = forward_x(wide(XX)) + by(XY) + backward_z(at(XZ), backward)
+        y = backward_x(wide(XY)) + fy(YY) + backward_z(at(YZ), backward)
+        z = backward_x(wide(XZ)) + by(YZ) + forward_z(at(ZZ), forward)
         for c, value in enumerate((x, y, z)):
-            result = before[c] + scale * value
-            new[c, own, pl.ds(base, 8), :] = result
-            if out is not None:
+            if halos:
+                result = old[c, own, pl.ds(base, 8), :] + scale * value
+                new[c, own, pl.ds(base, 8), :] = result
                 out[c, :, here, :] = result
-
-    def stress_rows(i, old, velocity, new, last):
-        base = pl.multiple_of(PAD + i * 8, 8)
-        here = pl.ds(pl.multiple_of(i * 8, 8), 8)
-
-        def at(c, layers, shift=0):
-            return velocity[c, layers, pl.ds(base + shift, 8), :]
+            else:
+                new[c, :, here, :] = old[c, :, here, :] + scale * value
+
+    def stress_group(g, old, velocity, new, last):
+        here, base = place(g)
+
+        def at(c, shift=0):
+            return velocity[c, own, pl.ds(base + shift, 8), :]
 
         def fy(c):
-            return NEAR_COEF * (at(c, own, 1) - at(c, own)) + FAR_COEF * (at(c, own, 2) - at(c, own, -1))
-
-        def by(c):
-            return NEAR_COEF * (at(c, own) - at(c, own, -1)) + FAR_COEF * (at(c, own, 1) - at(c, own, -2))
-
-        def fx(c):
-            return forward_x(at(c, pl.ds(LAY - 1, cx + 3)))
-
-        strain_x = backward_x(at(0, pl.ds(LAY - 2, cx + 3)))
-        strain_y = by(1)
-        strain_z = backward_z(at(2, own), backward)
-        shear = TIME_STEP * mu[:, here, :]
-        volume = TIME_STEP * lam[:, here, :] * (strain_x + strain_y + strain_z)
+            return near_far(at(c, 1), at(c), at(c, 2), at(c, -1))
+
+        strain_x = backward_x(outer_x(at(0)))
+        strain_y = near_far(at(1), at(1, -1), at(1, 1), at(1, -2))
+        strain_z = backward_z(at(2), backward)
+        shear = mu[own, here, :]
+        double = 2.0 * shear
+        volume = lam[:, here, :] * (strain_x + strain_y + strain_z)
         change = {
-            XX: volume + 2.0 * shear * strain_x,
-            YY: volume + 2.0 * shear * strain_y,
-            ZZ: volume + 2.0 * shear * strain_z,
-            XY: shear * (fy(0) + fx(1)),
-            XZ: shear * (forward_z(at(0, own), forward) + fx(2)),
-            YZ: shear * (forward_z(at(1, own), forward) + fy(2)),
+            XX: volume + double * strain_x,
+            YY: volume + double * strain_y,
+            ZZ: volume + double * strain_z,
+            XY: shear * (fy(0) + forward_x(outer_x(at(1)))),
+            XZ: shear * (forward_z(at(0), forward) + forward_x(outer_x(at(2)))),
+            YZ: shear * (forward_z(at(1), forward) + fy(2)),
         }
         for c, value in change.items():
             result = old[c, own, pl.ds(base, 8), :] + value
@@ -345,19 +383,116 @@
             else:
                 new[c, own, pl.ds(base, 8), :] = result
 
-    def each(function, *args):
-        def body(i, carry):
-            function(i, *args)
+    forward_halo = {0: ((1, -FAR_COEF),), 2: ((6, FAR_COEF),), 3: ((6, NEAR_COEF), (7, FAR_COEF))}
+    backward_halo = {0: ((1, -NEAR_COEF), (0, -FAR_COEF)), 1: ((1, -FAR_COEF),), 3: ((6, FAR_COEF),)}
+
+    def weighted(field, c, terms, rows):
+        total = None
+        for layer, coef in terms:
+            term = coef * field[c, layer, rows, :]
+            total = term if total is None else total + term
+        return total
+
+    def velocity_halo(g, stress, partial, new):
+        here, base = place(g)
+        rows = pl.ds(base, 8)
+        for c, (part, terms) in enumerate(((XX, forward_halo), (XY, backward_halo), (XZ, backward_halo))):
+            for layer in range(cx):
+                value = partial[c, layer, here, :]
+                if layer in terms:
+                    value = value + buo[layer, here, :] * weighted(stress, part, terms[layer], rows)
+                new[c, low + layer, rows, :] = value
+
+    def stress_halo(g, partial, velocity, new, last):
+        here, base = place(g)
+        rows = pl.ds(base, 8)
+
+        def add(c, layer, value):
+            if last:
+                if value is not None:
+                    new[SOURCE[c], layer, here, :] = new[SOURCE[c], layer, here, :] + value
+            else:
+                before = partial[c, low + layer, rows, :]
+                new[c, low + layer, rows, :] = before if value is None else before + value
+
+        for layer in range(cx):
+            if layer in backward_halo:
+                strain = weighted(velocity, 0, backward_halo[layer], rows)
+                volume = lam[layer, here, :] * strain
+                add(XX, layer, stiff[low + layer, here, :] * strain)
+                add(YY, layer, volume)
+                add(ZZ, layer, volume)
+            else:
+                for c in (XX, YY, ZZ):
+                    add(c, layer, None)
+            for c, part in ((XY, 1), (XZ, 2)):
+                if layer in forward_halo:
+                    add(c, layer, mu[low + layer, here, :] * weighted(velocity, part, forward_halo[layer], rows))
+                else:
+                    add(c, layer, None)
+            add(YZ, layer, None)
+        if last:
+            return
+        first, second, beneath, top = low, low + 1, high - 2, high - 1
+
+        def complete(c, layer, coefs, part, terms):
+            new[c, layer, rows, :] = partial[c, layer, rows, :] + coefs[layer, here, :] * weighted(velocity, part, terms, rows)
+
+        complete(XX, 1, stiff, 0, ((first, FAR_COEF),))
+        complete(XX, high, stiff, 0, ((top, -NEAR_COEF), (beneath, -FAR_COEF)))
+        complete(XX, high + 1, stiff, 0, ((top, -FAR_COEF),))
+        for c, part in ((XY, 1), (XZ, 2)):
+            complete(c, 0, mu, part, ((first, FAR_COEF),))
+            complete(c, 1, mu, part, ((first, NEAR_COEF), (second, FAR_COEF)))
+            complete(c, high, mu, part, ((top, -FAR_COEF),))
+
+    def each(first, last, function, *args):
+        def body(g, carry):
+            function(g, *args)
             return carry
 
-        lax.fori_loop(0, cy // 8, body, 0)
-
-    y_s0.wait_recv()
-    arrive(x_s0)
-    each(velocity_rows, v0, s0, v1)
-    x_v1, y_v1 = x_copies(1, v1), y_copy(1, v1)
-    start(x_v1)
-    y_v1.start()
+        lax.fori_loop(first, last, body, 0)
+
+    def each_edge_first(first, last, copy, function, *args):
+        def body(p, carry):
+            function(jnp.where(p == first, last - 1, p - 1), *args)
+
+            @pl.when(p == first)
+            def _():
+                copy.start()
+
+            return carry
+
+        lax.fori_loop(first, last, body, 0)
+
+    def each_edge_last(first, last, copy, function, *args):
+        def body(g, carry):
+            @pl.when(g == last - 1)
+            def _():
+                copy.wait_recv()
+
+            function(g, *args)
+            return carry
+
+        lax.fori_loop(first, last, body, 0)
+
+    each_edge_last(0, groups, y_s0, velocity_group, v0, s0, v0, False)
+    x_v1, y_v1 = chunks(V1, v1, s0_bounds), y_copy(1, v1)
+    x_sp, y_s1 = chunks(SP, sp, sp_bounds), y_copy(2, s1)
+    parts = len(s0_bounds) - 1
+    for i in range(parts):
+        final = i == parts - 1
+        arrive(x_s0[i])
+        if final:
+            each_edge_first(s0_bounds[i], groups, y_v1, velocity_halo, s0, v0, v1)
+        else:
+            each(s0_bounds[i], s0_bounds[i + 1], velocity_halo, s0, v0, v1)
+        start(x_v1[i])
+        if final:
+            each_edge_last(sp_bounds[i], groups, y_v1, stress_group, s0, v1, sp, False)
+        elif sp_bounds[i] < sp_bounds[i + 1]:
+            each(sp_bounds[i], sp_bounds[i + 1], stress_group, s0, v1, sp, False)
+        start(x_sp[i])
 
     for copy in ocean_loads:
         copy.wait()
@@ -390,13 +525,6 @@
     slot = lax.broadcasted_iota(jnp.int32, (8, 128), 0)
     picked = lanes_of(0).astype(jnp.int32) - tile + FAR_REACH == slot
     row[...] = jnp.where(picked, OCEAN_STEP * lanes_of(1), 0.0)
-
-    y_v1.wait_recv()
-    arrive(x_v1)
-    each(stress_rows, s0, v1, s1, False)
-    x_s1, y_s1 = x_copies(2, s1), y_copy(2, s1)
-    start(x_s1)
-    y_s1.start()
 
     for copy in y_ocean:
         copy.wait()
@@ -439,11 +567,21 @@
     ).astype(jnp.float32)
     vel1[2, here, :] = (oce[0, here, :] - ocean_fall(5, ocx + 6)) * mask_here
 
-    y_s1.wait_recv()
-    arrive(x_s1)
-    each(velocity_rows, v1, s1, v2, vel_out)
-    x_v2, y_v2 = x_copies(3, v2), y_copy(3, v2)
-    start(x_v2)
+    arrive(x_static)
+    x_v2, y_v2 = chunks(V2, v2, v2_bounds), y_copy(3, v2)
+    for i in range(parts):
+        final = i == parts - 1
+        arrive(x_v1[i])
+        arrive(x_sp[i])
+        if final:
+            each_edge_first(sp_bounds[i], groups, y_s1, stress_halo, sp, v1, s1, False)
+            each_edge_last(v2_bounds[i], groups, y_s1, velocity_group, v1, s1, v2, True, vel_out)
+        else:
+            if sp_bounds[i] < sp_bounds[i + 1]:
+                each(sp_bounds[i], sp_bounds[i + 1], stress_halo, sp, v1, s1, False)
+            if v2_bounds[i] < v2_bounds[i + 1]:
+                each(v2_bounds[i], v2_bounds[i + 1], velocity_group, v1, s1, v2, True, vel_out)
+        start(x_v2[i])
     y_v2.start()
 
     top = v2[2, own, rows_own, :].reshape(cx * cy, nz)
@@ -473,9 +611,10 @@
         pl.when(ahead)(copy.start)
     pat[FAR_REACH : FAR_REACH + 1, 0:ocy] = patch[0:1]
 
-    y_v2.wait_recv()
-    arrive(x_v2)
-    each(stress_rows, s1, v2, str_out, True)
+    each_edge_last(0, groups, y_v2, stress_group, s1, v2, str_out, True)
+    for i in range(parts):
+        arrive(x_v2[i])
+    each(0, groups, stress_halo, None, v2, str_out, True)
 
     for copy, ahead, back in patch_copies:
         pl.when(back)(copy.wait_recv)
@@ -489,7 +628,7 @@
     oce_out[0] = oce[0, orow_own, 0:ocy] - ocean_fall(PAD, ocx)[:, 0:ocy] + source[PAD : PAD + ocx, 0:ocy]
     oce_out[1:3] = oce[1:3, orow_own, 0:ocy]
 
-    for copies in (x_s0, x_ocean, x_v1, x_s1, x_v2):
+    for copies in (*x_s0, x_static, x_ocean, *x_v1, *x_sp, *x_v2):
         sent(copies)
     for copy in (y_s0, y_v1, y_s1, y_v2):
         copy.wait_send()
@@ -521,12 +660,14 @@
             scratch_shapes=[
                 pltpu.VMEM((6, layers, rows, nz), f32),
                 pltpu.VMEM((6, layers, rows, nz), f32),
+                pltpu.VMEM((6, layers, rows, nz), f32),
                 pltpu.VMEM(velocity.shape, f32),
                 pltpu.VMEM((3, layers, rows, nz), f32),
                 pltpu.VMEM((3, layers, rows, nz), f32),
                 pltpu.VMEM(buoyancy.shape, f32),
                 pltpu.VMEM(buoyancy.shape, f32),
-                pltpu.VMEM(buoyancy.shape, f32),
+                pltpu.VMEM((layers, cy, nz), f32),
+                pltpu.VMEM((layers, cy, nz), f32),
                 pltpu.VMEM((1, ocx), jnp.int32),
                 pltpu.VMEM((1, ocx), f32),
                 pltpu.VMEM((3, *region), f32),
@@ -539,8 +680,8 @@
                 pltpu.VMEM((2, *region), f32),
                 pltpu.VMEM((4, *region), f32),
                 dma((15,)),
-                dma((4, 2, 2)),
-                dma((4, 2, 2)),
+                dma((5, len(BOUNDS) - 1, 2, 2)),
+                dma((5, len(BOUNDS) - 1, 2, 2)),
                 dma((4,)),
                 dma((4,)),
                 dma((3, 4)),

time: 56 us -> 50.5 us (0.902); the launches traced: 55.2 us -> 50.3 us
  Pallas kernels: 52.2 us -> 47.4 us
    pallas_call x1, Pallas kernels: 52.2 us -> 47.4 us  [shards(): pl.pallas_call(functools.partial(kernel, tiles), out_shape=(jax.ShapeDtyp...]
where the time goes in v2:
time: 50.5 us; the launch traced here: 50.3 us
  Pallas kernels  47.4 us (94%)
  local copies, waits for them, and re-layouts  2.3 us (5%)
  between operations  0.64 us (1%)
    pallas_call x1, Pallas kernels, shards(): pl.pallas_call(functools.partial(kernel, tiles), out_shape=(jax.ShapeDtyp...  47.4 us
    unnamed x3, local copies, waits for them, and re-layouts  2.3 us

profile of v2, /device:TPU:9, one launch (start us, length us, event | category | flops | bytes accessed | tf_op | source)
XLA Modules:
  0.0 50.3 jit_solution(10899706510933361046)
XLA Ops:
  0.6 47.4 %shard_map.121 = (f32[3,4,64,128]{3,2,1,0:T(8,128)S(1)}, f32[6,4,64,128]{3,2,1,0:T(8,128)S(1)}, f32[3,64,256]{2,1,0:T(8,128)S(1)}) custom-call(f32[3,4,64,128]{3,2,1,0:T(8,128)} %vel_in.1, f32[6,4,64,128]{3,2,1,0:T(8,128)} %str_in.1, f32[4,64,128]{2,1,0:T(8,128)} %buo_in.1, f32[4,64,128]{2,1,0:T(8,128)} %lam_in.1, f32[4,64,128]{2,1,0:T(8,128)} %mu_in.1, ...), custom_call_target="tpu_custom_call" | custom-call | tf_op jit(solution)/shard_map/pallas_call | solution.py:651
  48.0 0.7 %copy.16 = f32[3,4,64,128]{3,2,1,0:T(8,128)} copy(f32[3,4,64,128]{3,2,1,0:T(8,128)S(1)} %get-tuple-element.6) | data formatting | bytes 786432
  48.8 0.9 %copy.17 = f32[6,4,64,128]{3,2,1,0:T(8,128)} copy(f32[6,4,64,128]{3,2,1,0:T(8,128)S(1)} %get-tuple-element.7) | data formatting | bytes 1572864
  49.6 0.7 %copy.18 = f32[3,64,256]{2,1,0:T(8,128)} copy(f32[3,64,256]{2,1,0:T(8,128)S(1)} %get-tuple-element.8) | data formatting | bytes 393216

commit v3 on v2

--- a/solution.py
+++ b/solution.py
@@ -71,7 +71,7 @@
     vel_out, str_out, oce_out,
     s0, sp, s1, v0, v1, v2, buo, lam, mu, stiff,
     src, share, oce, dep, wet, loc, locn, pat, row, flux, vel1,
-    load_sem, xs_sem, xr_sem, ys_sem, yr_sem, os_sem, or_sem, ps_sem, pr_sem,
+    load_sem, row_sem, xs_sem, xr_sem, ys_sem, yr_sem, os_sem, or_sem, ps_sem, pr_sem,
 ):
     cx, cy, nz = buo_in.shape
     ocx, ocy = dep_in.shape
@@ -88,53 +88,30 @@
         return {"sec": 1 - sec if other else sec, "tile": tile + step}
 
     loads = [
-        pltpu.make_async_copy(str_in.at[SOURCE[c]], s0.at[c, own, rows_own], load_sem.at[c])
+        pltpu.make_async_copy(str_in.at[SOURCE[c]], s0.at[c, own, rows_own], load_sem.at[0])
         for c in range(6)
     ]
     loads += [
-        pltpu.make_async_copy(vel_in, v0, load_sem.at[6]),
-        pltpu.make_async_copy(buo_in, buo, load_sem.at[7]),
-        pltpu.make_async_copy(lam_in, lam, load_sem.at[8]),
-        pltpu.make_async_copy(mu_in, mu.at[own], load_sem.at[9]),
+        pltpu.make_async_copy(vel_in, v0, load_sem.at[0]),
+        pltpu.make_async_copy(buo_in, buo, load_sem.at[0]),
+        pltpu.make_async_copy(lam_in, lam, load_sem.at[0]),
+        pltpu.make_async_copy(mu_in, mu.at[own], load_sem.at[0]),
     ]
     ocean_loads = [
-        pltpu.make_async_copy(oce_in, oce.at[:, orow_own, 0:ocy], load_sem.at[10]),
-        pltpu.make_async_copy(dep_in, dep.at[orow_own, 0:ocy], load_sem.at[11]),
-        pltpu.make_async_copy(wet_in, wet.at[orow_own, 0:ocy], load_sem.at[12]),
+        pltpu.make_async_copy(oce_in, oce.at[:, orow_own, 0:ocy], load_sem.at[1]),
+        pltpu.make_async_copy(dep_in, dep.at[orow_own, 0:ocy], load_sem.at[1]),
+        pltpu.make_async_copy(wet_in, wet.at[orow_own, 0:ocy], load_sem.at[1]),
     ]
     row_loads = [
-        pltpu.make_async_copy(src_in, src, load_sem.at[13]),
-        pltpu.make_async_copy(share_in, share, load_sem.at[14]),
+        pltpu.make_async_copy(src_in, src, row_sem.at[0]),
+        pltpu.make_async_copy(share_in, share, row_sem.at[1]),
     ]
-    for copy in row_loads + loads + ocean_loads:
-        copy.start()
-
-    outer = pl.multiple_of((cy + PAD) * sec, 8)
-    for field in (s0, s1):
-        field[0:3, own, pl.ds(outer, PAD), :] = jnp.zeros((3, cx, PAD, nz), jnp.float32)
-    for field in (v1, v2):
-        field[:, own, pl.ds(outer, PAD), :] = jnp.zeros((3, cx, PAD, nz), jnp.float32)
+
+    def wait_for(sem, *sizes):
+        part = s0.at[tuple(pl.ds(0, size) for size in sizes)]
+        pltpu.make_async_copy(part, part, sem).wait()
+
     pat[...] = jnp.zeros(pat.shape, jnp.float32)
-
-    def clear(layers, orow, slot):
-        for field in (s0, sp):
-            field[XY : XX + 1, layers, rows_own, :] = jnp.zeros((3, LAY, cy, nz), jnp.float32)
-        for field in (v1, v2):
-            field[:, layers, rows_own, :] = jnp.zeros((3, LAY, cy, nz), jnp.float32)
-        for field in (mu, stiff):
-            field[layers] = jnp.zeros((LAY, cy, nz), jnp.float32)
-        oce[:, orow, 0:ocy] = jnp.zeros((3, PAD, ocy), jnp.float32)
-        dep[orow, 0:ocy] = jnp.zeros((PAD, ocy), jnp.float32)
-        wet[orow, 0:ocy] = jnp.zeros((PAD, ocy), jnp.int32)
-        locn[slot] = jnp.zeros(locn.shape[1:], jnp.float32)
-
-    @pl.when(jnp.logical_not(has_low))
-    def _():
-        clear(slice(0, LAY), slice(0, PAD), 0)
-
-    @pl.when(jnp.logical_not(has_high))
-    def _():
-        clear(slice(LAY + cx, LAY + cx + LAY), slice(PAD + ocx, PAD + ocx + PAD), 1)
 
     barrier = pltpu.get_barrier_semaphore()
     pl.semaphore_signal(barrier, inc=1, device_id=device(0, True), device_id_type=MESH)
@@ -169,10 +146,11 @@
         return pl.multiple_of(8 * first + sec * (cy - 8 * first - 8 * last), 8), 8 * (last - first)
 
     S0, V1, SP, V2, STATIC = range(5)
+    LAYERS = ((5, 4), (4, 5), (5, 4), (4, 5), (3, 3))
 
     def x_copies(number, field, chunk=0, first=0, last=groups, source=None):
         if first == last:
-            return [], []
+            return [], [], 0, None
         begin, count = rows_of(first, last)
         rows = pl.ds(PAD + begin, count)
         if number in (S0, SP):
@@ -205,14 +183,14 @@
             ups = [(stiff.at[high - 1 : high], stiff.at[1:2]), (mu.at[high - 2 : high], mu.at[0:2])]
             downs = [(stiff.at[low : low + 2], stiff.at[high : high + 2]), (mu.at[low : low + 1], mu.at[high : high + 1])]
         up = [
-            copy_to(a, b, xs_sem.at[number, chunk, 0, i], xr_sem.at[number, chunk, 0, i], device(1))
-            for i, (a, b) in enumerate(ups)
+            copy_to(a, b, xs_sem.at[0], xr_sem.at[number, chunk, 0], device(1))
+            for a, b in ups
         ]
         down = [
-            copy_to(a, b, xs_sem.at[number, chunk, 1, i], xr_sem.at[number, chunk, 1, i], device(-1))
-            for i, (a, b) in enumerate(downs)
+            copy_to(a, b, xs_sem.at[1], xr_sem.at[number, chunk, 1], device(-1))
+            for a, b in downs
         ]
-        return up, down
+        return up, down, count, [xr_sem.at[number, chunk, d] for d in range(2)] + [LAYERS[number]]
 
     def chunks(number, field, bounds, source=None):
         return [
@@ -221,7 +199,7 @@
         ]
 
     def start(copies):
-        up, down = copies
+        up, down = copies[:2]
 
         @pl.when(has_high)
         def _():
@@ -234,30 +212,21 @@
                 copy.start()
 
     def arrive(copies):
-        up, down = copies
+        count = copies[2]
+        if count == 0:
+            return
+        from_low, from_high, layers = copies[3]
 
         @pl.when(has_low)
         def _():
-            for copy in up:
-                copy.wait_recv()
+            wait_for(from_low, 1, layers[0], count)
 
         @pl.when(has_high)
         def _():
-            for copy in down:
-                copy.wait_recv()
-
-    def sent(copies):
-        up, down = copies
-
-        @pl.when(has_high)
-        def _():
-            for copy in up:
-                copy.wait_send()
-
-        @pl.when(has_low)
-        def _():
-            for copy in down:
-                copy.wait_send()
+            wait_for(from_high, 1, layers[1], count)
+
+    def ocean_wait(sem):
+        wait_for(sem, 1, 2, (5 * PAD * ocy // nz + 2 * PAD) // 2)
 
     y_from = pl.multiple_of(cy - (cy - PAD) * sec, 8)
     y_to = pl.multiple_of((cy + PAD) * sec, 8)
@@ -267,12 +236,40 @@
         return copy_to(
             part.at[:, :, pl.ds(y_from, PAD)],
             part.at[:, :, pl.ds(y_to, PAD)],
-            ys_sem.at[number], yr_sem.at[number], device(0, True),
+            ys_sem.at[0], yr_sem.at[number], device(0, True),
         )
 
     x_s0 = chunks(S0, s0, s0_bounds, str_in)
     for part in x_s0:
         start(part)
+    for copy in row_loads + loads + ocean_loads:
+        copy.start()
+
+    outer = pl.multiple_of((cy + PAD) * sec, 8)
+    for field in (s0, s1):
+        field[0:3, own, pl.ds(outer, PAD), :] = jnp.zeros((3, cx, PAD, nz), jnp.float32)
+    for field in (v1, v2):
+        field[:, own, pl.ds(outer, PAD), :] = jnp.zeros((3, cx, PAD, nz), jnp.float32)
+
+    def clear(layers, orow, slot):
+        for field in (s0, sp):
+            field[XY : XX + 1, layers, rows_own, :] = jnp.zeros((3, LAY, cy, nz), jnp.float32)
+        for field in (v1, v2):
+            field[:, layers, rows_own, :] = jnp.zeros((3, LAY, cy, nz), jnp.float32)
+        for field in (mu, stiff):
+            field[layers] = jnp.zeros((LAY, cy, nz), jnp.float32)
+        oce[:, orow, 0:ocy] = jnp.zeros((3, PAD, ocy), jnp.float32)
+        dep[orow, 0:ocy] = jnp.zeros((PAD, ocy), jnp.float32)
+        wet[orow, 0:ocy] = jnp.zeros((PAD, ocy), jnp.int32)
+        locn[slot] = jnp.zeros(locn.shape[1:], jnp.float32)
+
+    @pl.when(jnp.logical_not(has_low))
+    def _():
+        clear(slice(0, LAY), slice(0, PAD), 0)
+
+    @pl.when(jnp.logical_not(has_high))
+    def _():
+        clear(slice(LAY + cx, LAY + cx + LAY), slice(PAD + ocx, PAD + ocx + PAD), 1)
 
     loc[...] = jnp.zeros(loc.shape, jnp.float32)
     for copy in row_loads:
@@ -282,18 +279,17 @@
 
     def ocean_rows(step, first, target, slot, index):
         return [
-            copy_to(oce_in.at[:, pl.ds(first, PAD)], oce.at[:, pl.ds(target, PAD), 0:ocy], os_sem.at[index, 0], or_sem.at[index, 0], device(step)),
-            copy_to(dep_in.at[pl.ds(first, PAD)], dep.at[pl.ds(target, PAD), 0:ocy], os_sem.at[index, 1], or_sem.at[index, 1], device(step)),
-            copy_to(wet_in.at[pl.ds(first, PAD)], wet.at[pl.ds(target, PAD), 0:ocy], os_sem.at[index, 2], or_sem.at[index, 2], device(step)),
-            copy_to(loc, locn.at[slot], os_sem.at[index, 3], or_sem.at[index, 3], device(step)),
+            copy_to(oce_in.at[:, pl.ds(first, PAD)], oce.at[:, pl.ds(target, PAD), 0:ocy], os_sem.at[index], or_sem.at[index], device(step)),
+            copy_to(dep_in.at[pl.ds(first, PAD)], dep.at[pl.ds(target, PAD), 0:ocy], os_sem.at[index], or_sem.at[index], device(step)),
+            copy_to(wet_in.at[pl.ds(first, PAD)], wet.at[pl.ds(target, PAD), 0:ocy], os_sem.at[index], or_sem.at[index], device(step)),
+            copy_to(loc, locn.at[slot], os_sem.at[index], or_sem.at[index], device(step)),
         ]
 
     x_ocean = (
         ocean_rows(1, ocx - PAD, 0, 0, 0),
         ocean_rows(-1, 0, PAD + ocx, 1, 1),
     )
-    for copy in loads:
-        copy.wait()
+    wait_for(load_sem.at[0], 6, 2 * cx, cy)
     y_s0 = y_copy(0, s0)
     y_s0.start()
 
@@ -494,20 +490,17 @@
             each(sp_bounds[i], sp_bounds[i + 1], stress_group, s0, v1, sp, False)
         start(x_sp[i])
 
-    for copy in ocean_loads:
-        copy.wait()
-    arrive(x_ocean)
+    wait_for(load_sem.at[1], 5, ocx * ocy // (nz * cy), cy)
+    pl.when(has_low)(lambda: ocean_wait(or_sem.at[0]))
+    pl.when(has_high)(lambda: ocean_wait(or_sem.at[1]))
     edge = pl.multiple_of(half * (1 - sec), 128)
 
-    def ocean_columns(field, index):
-        part = field.at[:, :, :] if len(field.shape) == 3 else field.at[:, :]
-        if len(field.shape) == 3:
-            a, b = part.at[:, :, pl.ds(edge, half)], part.at[:, :, ocy : ocy + half]
-        else:
-            a, b = part.at[:, pl.ds(edge, half)], part.at[:, ocy : ocy + half]
-        return copy_to(a, b, os_sem.at[2, index], or_sem.at[2, index], device(0, True))
-
-    y_ocean = [ocean_columns(oce, 0), ocean_columns(dep, 1), ocean_columns(wet, 2)]
+    def ocean_columns(field):
+        where = (slice(None),) * (len(field.shape) - 1)
+        a, b = field.at[(*where, pl.ds(edge, half))], field.at[(*where, pl.ds(ocy, half))]
+        return copy_to(a, b, os_sem.at[2], or_sem.at[2], device(0, True))
+
+    y_ocean = [ocean_columns(oce), ocean_columns(dep), ocean_columns(wet)]
     for copy in y_ocean:
         copy.start()
 
@@ -526,8 +519,8 @@
     picked = lanes_of(0).astype(jnp.int32) - tile + FAR_REACH == slot
     row[...] = jnp.where(picked, OCEAN_STEP * lanes_of(1), 0.0)
 
-    for copy in y_ocean:
-        copy.wait()
+    for sem in (or_sem.at[2], os_sem.at[2]):
+        wait_for(sem, 1, 5, ocx + 2 * PAD)
     region = oce.shape[1:]
     width = region[1]
     lanes = lax.broadcasted_iota(jnp.int32, (1, width), 1)
@@ -628,12 +621,30 @@
     oce_out[0] = oce[0, orow_own, 0:ocy] - ocean_fall(PAD, ocx)[:, 0:ocy] + source[PAD : PAD + ocx, 0:ocy]
     oce_out[1:3] = oce[1:3, orow_own, 0:ocy]
 
-    for copies in (*x_s0, x_static, x_ocean, *x_v1, *x_sp, *x_v2):
-        sent(copies)
-    for copy in (y_s0, y_v1, y_s1, y_v2):
-        copy.wait_send()
+    @pl.when(has_high)
+    def _():
+        wait_for(xs_sem.at[0], 3, 7, cy)
+        ocean_wait(os_sem.at[0])
+
+    @pl.when(has_low)
+    def _():
+        wait_for(xs_sem.at[1], 3, 7, cy)
+        ocean_wait(os_sem.at[1])
+
+    wait_for(ys_sem.at[0], 6, 8, 2 * cx)
     for copy, ahead, back in patch_copies:
         pl.when(ahead)(copy.wait_send)
+
+
+def store(velocity, stresses, ocean, vel_out, str_out, oce_out, sem):
+    copies = [
+        pltpu.make_async_copy(a, b, sem.at[i])
+        for i, (a, b) in enumerate(((stresses, str_out), (velocity, vel_out), (ocean, oce_out)))
+    ]
+    for copy in copies:
+        copy.start()
+    for copy in copies:
+        copy.wait()
 
 
 def solution(mesh):
@@ -648,7 +659,7 @@
         vmem = pl.BlockSpec(memory_space=pltpu.VMEM)
         dma = pltpu.SemaphoreType.DMA
         f32 = jnp.float32
-        return pl.pallas_call(
+        results = pl.pallas_call(
             functools.partial(kernel, tiles),
             out_shape=(
                 jax.ShapeDtypeStruct(velocity.shape, f32),
@@ -673,19 +684,20 @@
                 pltpu.VMEM((3, *region), f32),
                 pltpu.VMEM(region, f32),
                 pltpu.VMEM(region, jnp.int32),
-                pltpu.VMEM((8, 128), f32),
-                pltpu.VMEM((2, 8, 128), f32),
+                pltpu.VMEM((2 * PAD, 128), f32),
+                pltpu.VMEM((2, 2 * PAD, 128), f32),
                 pltpu.VMEM((16, region[1]), f32),
                 pltpu.VMEM((8, 128), f32),
                 pltpu.VMEM((2, *region), f32),
                 pltpu.VMEM((4, *region), f32),
-                dma((15,)),
-                dma((5, len(BOUNDS) - 1, 2, 2)),
-                dma((5, len(BOUNDS) - 1, 2, 2)),
+                dma((2,)),
+                dma((2,)),
+                dma((2,)),
+                dma((5, len(BOUNDS) - 1, 2)),
+                dma((1,)),
                 dma((4,)),
-                dma((4,)),
-                dma((3, 4)),
-                dma((3, 4)),
+                dma((3,)),
+                dma((3,)),
                 dma((2, 7)),
                 dma((2, 7)),
             ],
@@ -701,6 +713,14 @@
                 )
             )
         )
+        return pl.pallas_call(
+            store,
+            out_shape=tuple(jax.ShapeDtypeStruct(r.shape, f32) for r in results),
+            in_specs=[vmem] * 3,
+            out_specs=(hbm,) * 3,
+            scratch_shapes=[dma((3,))],
+            compiler_params=pltpu.CompilerParams(vmem_limit_bytes=8 * 1024 * 1024),
+        )(*results)
 
     return jax.shard_map(
         shards,

time: 50.5 us -> 48.5 us (0.960)
  local copies, waits for them, and re-layouts: 2.3 us -> 0 us
    unnamed x3 -> x0, local copies, waits for them, and re-layouts: 2.3 us -> none
    pallas_call x0 -> x1, Pallas kernels: none -> 1.09 us  [shards(): pl.pallas_call(store, out_shape=tuple((jax.ShapeDtypeStruct(r.shape, f32)...]
    pallas_call x1, Pallas kernels: 47.4 us -> 46.6 us  [shards(): pl.pallas_call(functools.partial(kernel, tiles), out_shape=(jax.ShapeDtyp...]
where the time goes in v3:
time: 48.5 us; the launch traced here: 48.3 us
  Pallas kernels  47.7 us (98%)
  between operations  0.64 us (1%)
    pallas_call x1, Pallas kernels, shards(): pl.pallas_call(functools.partial(kernel, tiles), out_shape=(jax.ShapeDtyp...  46.6 us
    pallas_call x1, Pallas kernels, shards(): pl.pallas_call(store, out_shape=tuple((jax.ShapeDtypeStruct(r.shape, f32)...  1.09 us

profile of v3, /device:TPU:9, one launch (start us, length us, event | category | flops | bytes accessed | tf_op | source)
XLA Modules:
  0.0 48.3 jit_solution(7654573605311816923)
XLA Ops:
  0.6 46.6 %shard_map.121 = (f32[3,4,64,128]{3,2,1,0:T(8,128)S(1)}, f32[6,4,64,128]{3,2,1,0:T(8,128)S(1)}, f32[3,64,256]{2,1,0:T(8,128)S(1)}) custom-call(f32[3,4,64,128]{3,2,1,0:T(8,128)} %vel_in.1, f32[6,4,64,128]{3,2,1,0:T(8,128)} %str_in.1, f32[4,64,128]{2,1,0:T(8,128)} %buo_in.1, f32[4,64,128]{2,1,0:T(8,128)} %lam_in.1, f32[4,64,128]{2,1,0:T(8,128)} %mu_in.1, ...), custom_call_target="tpu_custom_call" | custom-call | tf_op jit(solution)/shard_map/pallas_call | solution.py:662
  47.2 1.1 %shard_map.122 = (f32[3,4,64,128]{3,2,1,0:T(8,128)}, f32[6,4,64,128]{3,2,1,0:T(8,128)}, f32[3,64,256]{2,1,0:T(8,128)}) custom-call(f32[3,4,64,128]{3,2,1,0:T(8,128)S(1)} %get-tuple-element.6.velocity, f32[6,4,64,128]{3,2,1,0:T(8,128)S(1)} %get-tuple-element.7.stresses, f32[3,64,256]{2,1,0:T(8,128)S(1)} %get-tuple-element.8.ocean), custom_call_target="tpu_custom_call" | custom-call | tf_op jit(solution)/shard_map/pallas_call | solution.py:716

commit v4 on v3

--- a/solution.py
+++ b/solution.py
@@ -20,7 +20,7 @@
 
 PAD = 8
 LAY = 2
-BOUNDS = (0, 4, 8)
+BOUNDS = (0, 7, 8)
 
 
 def lane_coefs(shape):

time: 48.5 us -> 47.3 us (0.975)
  Pallas kernels: 47.7 us -> 46.5 us
    pallas_call x1, Pallas kernels: 46.6 us -> 45.4 us  [shards(): pl.pallas_call(functools.partial(kernel, tiles), out_shape=(jax.ShapeDtyp...]
where the time goes in v4:
time: 47.3 us; the launch traced here: 47.1 us
  Pallas kernels  46.5 us (98%)
  between operations  0.64 us (1%)
    pallas_call x1, Pallas kernels, shards(): pl.pallas_call(functools.partial(kernel, tiles), out_shape=(jax.ShapeDtyp...  45.4 us
    pallas_call x1, Pallas kernels, shards(): pl.pallas_call(store, out_shape=tuple((jax.ShapeDtypeStruct(r.shape, f32)...  1.09 us

profile of v4, /device:TPU:9, one launch (start us, length us, event | category | flops | bytes accessed | tf_op | source)
XLA Modules:
  0.0 47.1 jit_solution(11415047828920497734)
XLA Ops:
  0.6 45.4 %shard_map.121 = (f32[3,4,64,128]{3,2,1,0:T(8,128)S(1)}, f32[6,4,64,128]{3,2,1,0:T(8,128)S(1)}, f32[3,64,256]{2,1,0:T(8,128)S(1)}) custom-call(f32[3,4,64,128]{3,2,1,0:T(8,128)} %vel_in.1, f32[6,4,64,128]{3,2,1,0:T(8,128)} %str_in.1, f32[4,64,128]{2,1,0:T(8,128)} %buo_in.1, f32[4,64,128]{2,1,0:T(8,128)} %lam_in.1, f32[4,64,128]{2,1,0:T(8,128)} %mu_in.1, ...), custom_call_target="tpu_custom_call" | custom-call | tf_op jit(solution)/shard_map/pallas_call | solution.py:662
  46.0 1.1 %shard_map.122 = (f32[3,4,64,128]{3,2,1,0:T(8,128)}, f32[6,4,64,128]{3,2,1,0:T(8,128)}, f32[3,64,256]{2,1,0:T(8,128)}) custom-call(f32[3,4,64,128]{3,2,1,0:T(8,128)S(1)} %get-tuple-element.6.velocity, f32[6,4,64,128]{3,2,1,0:T(8,128)S(1)} %get-tuple-element.7.stresses, f32[3,64,256]{2,1,0:T(8,128)S(1)} %get-tuple-element.8.ocean), custom_call_target="tpu_custom_call" | custom-call | tf_op jit(solution)/shard_map/pallas_call | solution.py:716
